TPU v7x, 128 devices: a whole 4x4x4 slice. The times are simulated.
128 devices in a mesh: gx: 16 (over z_hi, y, core), gy: 8 (over z_lo, x).
Axes of the slice: x: 4, y: 4, z: 4 (z_hi: 2, z_lo: 2; z = z_hi * 2 + z_lo), core: 2. Of those that a mesh axis runs over, the one named last changes fastest.
Arguments:
- resid_factor: float32 [8, 128, 128, 512], P(None, 'gx', 'gy'), may hold values from -8 to 8
- coefficients: float32 [6, 128, 128, 512], P(None, 'gx', 'gy'), may hold values from 0.2 to 2
- observer: bfloat16 [128, 128, 128, 512], P(None, 'gx', 'gy'), may hold values from -0.001953125 to 0.001953125
- shift_index: int32 [8], replicated, may hold values from 0 to 15
Outputs:
- factor: float32 [8, 128, 128, 512], P(None, 'gx', 'gy')
- new_resid: float32 [8, 128, 128, 512], P(None, 'gx', 'gy')
- gram: float32 [8, 128], replicated
- norms: float32 [8], replicated
All inputs are finite; a program needn't handle non-finite values.
Results may differ from a plain program's by a relative error of at most 0.0029.
Values sent between devices are 32-bit elements; how exact they have to be, the bound alone decides.
No kernel may reach another device: no remote copies, remote signals or barrier semaphores. Data moves between devices by JAX's collectives and lax.ppermute only.
A program may use at most 128 MiB of HBM per device.

v0:
```python
import jax
import jax.numpy as jnp
from jax import lax
from jax.sharding import PartitionSpec as P

COLS = 8
QCOLS = 128


def padded_2(cells, sides, width):
    for axis, dim in sides:
        count = lax.axis_size(axis)
        head = lax.slice_in_dim(cells, 0, width, axis=dim)
        tail = lax.slice_in_dim(cells, cells.shape[dim] - width, cells.shape[dim], axis=dim)
        cells = jnp.concatenate(
            [
                lax.ppermute(tail, axis, [(i, (i + 1) % count) for i in range(count)]),
                cells,
                lax.ppermute(head, axis, [((i + 1) % count, i) for i in range(count)]),
            ],
            axis=dim,
        )
    return cells


def shift_values(shift_index):
    return 0.2 * jnp.exp(jnp.log(40.0) * shift_index.astype(jnp.float32) / 15.0)


def spread(padded, coefficients):
    center = padded[:, 1:-1, 1:-1]
    zpadded = jnp.pad(center, ((0, 0), (0, 0), (0, 0), (1, 1)))
    total = coefficients[0] * padded[:, :-2, 1:-1] + coefficients[1] * padded[:, 2:, 1:-1]
    total = total + coefficients[2] * padded[:, 1:-1, :-2] + coefficients[3] * padded[:, 1:-1, 2:]
    total = total + coefficients[4] * zpadded[..., :-2] + coefficients[5] * zpadded[..., 2:]
    return total


def face_padded(field):
    return padded_2(field, (("gx", 1), ("gy", 2)), 1)


def chebyshev(jacobi, start, omega_two, omega_three):
    second = jacobi(start)
    third = start + omega_two * (jacobi(second) - start)
    return second + omega_three * (jacobi(third) - second)


def local(resid_factor, coefficients, observer, shift_index):
    sigma = shift_values(shift_index)[:, None, None, None]
    radius = 12.0 / (12.0 + sigma)
    omega_two = 1.0 / (1.0 - radius * radius / 2.0)
    omega_three = 1.0 / (1.0 - radius * radius * omega_two / 4.0)
    diagonal = jnp.sum(coefficients, axis=0)[None] + sigma

    def jacobi(field):
        return (resid_factor + spread(face_padded(field), coefficients)) / diagonal

    solved = chebyshev(jacobi, resid_factor / diagonal, omega_two, omega_three)
    factor = jnp.sqrt(2.0 * sigma) * solved
    new_resid = resid_factor - 2.0 * sigma * solved
    flat = factor.astype(jnp.bfloat16).reshape(COLS, -1)
    gram_part = lax.dot_general(
        flat,
        observer.reshape(QCOLS, -1),
        (((1,), (1,)), ((), ())),
        preferred_element_type=jnp.float32,
    )
    norm_part = jnp.sum(new_resid * new_resid, axis=(1, 2, 3))
    gram, norm_total = lax.psum((gram_part, norm_part), ("gx", "gy"))
    local_cells = resid_factor.shape[1] * resid_factor.shape[2] * resid_factor.shape[3]
    norms = norm_total / (local_cells * lax.axis_size("gx") * lax.axis_size("gy"))
    return (factor, new_resid, gram, norms)


def solution(mesh):
    placed = (P(None, "gx", "gy", None), P(None, "gx", "gy", None), P(None, "gx", "gy", None), P())
    return jax.shard_map(
        local,
        mesh=mesh,
        in_specs=placed,
        out_specs=(P(None, "gx", "gy", None), P(None, "gx", "gy", None), P(), P()),
        check_vma=False,
    )
```

profile of v0, /device:TPU:1, one launch (start us, length us, event | category | flops | bytes accessed | tf_op | source)
XLA Modules:
  0.0 185.1 jit_solution(10791084484284609969)
XLA Ops:
  1.3 1.6 reduce_sum.18
  2.9 3.0 %add_divide_fusion.3 = f32[8,8,16,512]{3,0,2,1:T(8,128)S(1)} fusion(f32[8,8,16,512]{3,2,1,0:T(8,128)} %param.4, f32[8]{0:T(128)S(1)} %get-tuple-element.35, f32[8,16,512]{2,1,0:T(8,128)S(1)} %reduce_sum.18), kind=kLoop, calls=%fused_computation.5 | loop fusion | flops 1048576 | bytes 4456480 | tf_op jit(solution)/shard_map/div | solution.py:59
  6.0 2.7 %collective-permute-start = (f32[8,1,16,512]{3,0,2,1:T(8,128)S(1)}, f32[8,1,16,512]{3,0,2,1:T(8,128)S(1)}, u32[]{:S(2)}, u32[]{:S(2)}) collective-permute-start(f32[8,1,16,512]{3,0,2,1:T(8,128)S(1)} %get-tuple-element.25), channel_id=1, source_target_pairs={{0,8},{8,16},{16,24},{24,32},{32,40},{40,48},{48,56},{56,64},{64,7... | collective-permute-start | bytes 786440 | tf_op jit(solution)/shard_map/ppermute | solution.py:17
  8.7 3.3 %collective-permute-done = f32[8,1,16,512]{3,0,2,1:T(8,128)S(1)} collective-permute-done((f32[8,1,16,512]{3,0,2,1:T(8,128)S(1)}, f32[8,1,16,512]{3,0,2,1:T(8,128)S(1)}, u32[]{:S(2)}, u32[]{:S(2)}) %collective-permute-start) | collective-permute-done | bytes 262176 | tf_op jit(solution)/shard_map/ppermute | solution.py:17
  12.1 2.8 %collective-permute-done.1 = f32[8,1,16,512]{3,0,2,1:T(8,128)S(1)} collective-permute-done((f32[8,1,16,512]{3,0,2,1:T(8,128)S(1)}, f32[8,1,16,512]{3,0,2,1:T(8,128)S(1)}, u32[]{:S(2)}, u32[]{:S(2)}) %collective-permute-start.1) | collective-permute-done | bytes 262176 | tf_op jit(solution)/shard_map/ppermute | solution.py:19
  14.9 1.3 collective-permute-start.2
  16.1 2.7 %collective-permute-start.3 = (f32[8,10,1,512]{3,0,2,1:T(8,128)S(1)}, f32[8,10,1,512]{3,0,2,1:T(8,128)S(1)}, u32[]{:S(2)}, u32[]{:S(2)}) collective-permute-start(f32[8,10,1,512]{3,0,2,1:T(8,128)S(1)} %get-tuple-element.20), channel_id=1, source_target_pairs={{1,0},{2,1},{3,2},{4,3},{5,4},{6,5},{7,6},{0,7},{9,8},{10,9},{11,1... | collective-permute-start | bytes 491528 | tf_op jit(solution)/shard_map/ppermute | solution.py:19
  19.0 2.4 %collective-permute-done.2 = f32[8,10,1,512]{3,0,2,1:T(8,128)S(1)} collective-permute-done((f32[8,10,1,512]{3,0,2,1:T(8,128)S(1)}, f32[8,10,1,512]{3,0,2,1:T(8,128)S(1)}, u32[]{:S(2)}, u32[]{:S(2)}) %collective-permute-start.2) | collective-permute-done | bytes 163872 | tf_op jit(solution)/shard_map/ppermute | solution.py:17
  21.5 5.5 %add_divide_fusion.2 = f32[8,8,16,512]{3,0,2,1:T(8,128)S(1)} fusion(f32[8,8,16,512]{3,0,2,1:T(8,128)S(1)} %add_divide_fusion.3, f32[8,10,1,512]{3,0,2,1:T(8,128)S(1)} %collective-permute-done.3, f32[8,1,16,512]{3,0,2,1:T(8,128)S(1)} %collective-permute-done.1, f32[8,1,16,512]{3,0,2,1:T(8,128)S(1)} %collective-permute-done, ...), kind=kLoop, calls=%fused_computation.4 | loop fusion | flops 11534336 | bytes 8978464 | tf_op jit(solution)/shard_map/div | solution.py:57
  27.1 1.4 collective-permute-start.4
  28.5 2.2 %collective-permute-start.5 = (f32[8,1,16,512]{3,0,2,1:T(8,128)S(1)}, f32[8,1,16,512]{3,0,2,1:T(8,128)S(1)}, u32[]{:S(2)}, u32[]{:S(2)}) collective-permute-start(f32[8,1,16,512]{3,0,2,1:T(8,128)S(1)} %get-tuple-element.24), channel_id=1, source_target_pairs={{8,0},{16,8},{24,16},{32,24},{40,32},{48,40},{56,48},{64,56},{72,6... | collective-permute-start | bytes 786440 | tf_op jit(solution)/shard_map/ppermute | solution.py:19
  31.8 2.5 %collective-permute-done.5 = f32[8,1,16,512]{3,0,2,1:T(8,128)S(1)} collective-permute-done((f32[8,1,16,512]{3,0,2,1:T(8,128)S(1)}, f32[8,1,16,512]{3,0,2,1:T(8,128)S(1)}, u32[]{:S(2)}, u32[]{:S(2)}) %collective-permute-start.5) | collective-permute-done | bytes 262176 | tf_op jit(solution)/shard_map/ppermute | solution.py:19
  35.5 3.1 %collective-permute-start.7 = (f32[8,10,1,512]{3,0,2,1:T(8,128)S(1)}, f32[8,10,1,512]{3,0,2,1:T(8,128)S(1)}, u32[]{:S(2)}, u32[]{:S(2)}) collective-permute-start(f32[8,10,1,512]{3,0,2,1:T(8,128)S(1)} %get-tuple-element.18), channel_id=1, source_target_pairs={{1,0},{2,1},{3,2},{4,3},{5,4},{6,5},{7,6},{0,7},{9,8},{10,9},{11,1... | collective-permute-start | bytes 491528 | tf_op jit(solution)/shard_map/ppermute | solution.py:19
  38.7 3.3 %collective-permute-done.6 = f32[8,10,1,512]{3,0,2,1:T(8,128)S(1)} collective-permute-done((f32[8,10,1,512]{3,0,2,1:T(8,128)S(1)}, f32[8,10,1,512]{3,0,2,1:T(8,128)S(1)}, u32[]{:S(2)}, u32[]{:S(2)}) %collective-permute-start.6) | collective-permute-done | bytes 163872 | tf_op jit(solution)/shard_map/ppermute | solution.py:17
  42.0 5.8 %multiply_add_fusion.1 = f32[8,8,16,512]{3,0,2,1:T(8,128)S(1)} fusion(f32[8,8,16,512]{3,0,2,1:T(8,128)S(1)} %add_divide_fusion.2, f32[8,10,1,512]{3,0,2,1:T(8,128)S(1)} %collective-permute-done.7, f32[8,1,16,512]{3,0,2,1:T(8,128)S(1)} %collective-permute-done.5, f32[8,1,16,512]{3,0,2,1:T(8,128)S(1)} %collective-permute-done.4, ...), kind=kLoop, calls=%fused_computation.77 | loop fusion | flops 13631488 | bytes 8978496 | tf_op jit(solution)/shard_map/add | solution.py:45
  48.5 5.0 %collective-permute-start.9 = (f32[8,1,16,512]{3,0,2,1:T(8,128)S(1)}, f32[8,1,16,512]{3,0,2,1:T(8,128)S(1)}, u32[]{:S(2)}, u32[]{:S(2)}) collective-permute-start(f32[8,1,16,512]{3,0,2,1:T(8,128)S(1)} %get-tuple-element.22), channel_id=1, source_target_pairs={{8,0},{16,8},{24,16},{32,24},{40,32},{48,40},{56,48},{64,56},{72,6... | collective-permute-start | bytes 786440 | tf_op jit(solution)/shard_map/ppermute | solution.py:19
  54.7 1.8 collective-permute-start.10
  56.5 2.4 %collective-permute-start.11 = (f32[8,10,1,512]{3,0,2,1:T(8,128)S(1)}, f32[8,10,1,512]{3,0,2,1:T(8,128)S(1)}, u32[]{:S(2)}, u32[]{:S(2)}) collective-permute-start(f32[8,10,1,512]{3,0,2,1:T(8,128)S(1)} %get-tuple-element.16), channel_id=1, source_target_pairs={{1,0},{2,1},{3,2},{4,3},{5,4},{6,5},{7,6},{0,7},{9,8},{10,9},{11,1... | collective-permute-start | bytes 491528 | tf_op jit(solution)/shard_map/ppermute | solution.py:19
  59.0 2.7 %collective-permute-done.10 = f32[8,10,1,512]{3,0,2,1:T(8,128)S(1)} collective-permute-done((f32[8,10,1,512]{3,0,2,1:T(8,128)S(1)}, f32[8,10,1,512]{3,0,2,1:T(8,128)S(1)}, u32[]{:S(2)}, u32[]{:S(2)}) %collective-permute-start.10) | collective-permute-done | bytes 163872 | tf_op jit(solution)/shard_map/ppermute | solution.py:17
  61.7 7.1 %multiply_reduce_fusion = (f32[8]{0:T(128)S(1)}, f32[8,8,16,512]{3,0,2,1:T(8,128)}, f32[8,8,16,512]{3,0,2,1:T(8,128)S(1)}) fusion(f32[8]{0:T(128)S(1)} %get-tuple-element.36, f32[8,8,16,512]{3,2,1,0:T(8,128)S(1)} %copy-done, f32[8,8,16,512]{3,0,2,1:T(8,128)S(1)} %add_divide_fusion.2, f32[8]{0:T(128)S(1)} %get-tuple-element.35, ...), kind=kLoop, calls=%fused_computation.74 | loop fusion | flops 15204344 | bytes 13172864 | tf_op jit(solution)/shard_map/reduce_sum | solution.py:69
  69.1 2.5 %copy.16 = f32[8,8,16,512]{3,2,1,0:T(8,128)} copy(f32[8,8,16,512]{3,0,2,1:T(8,128)S(1)} %broadcast_multiply_fusion) | data formatting | bytes 4194304
  71.6 29.1 %fusion.40 = f32[8,128]{1,0:T(8,128)S(1)} fusion(bf16[128,8,16,512]{3,2,1,0:T(8,128)(2,1)} %param.6, f32[8,8,16,512]{3,0,2,1:T(8,128)S(1)} %broadcast_multiply_fusion), kind=kOutput, calls=%fused_computation.78 | convolution fusion | flops 134742016 | bytes 18878464 | tf_op jit(solution)/shard_map/dot_general | solution.py:63
  100.7 79.7 %all-reduce.3 = (f32[8,128]{1,0:T(8,128)}, f32[8]{0:T(128)S(1)}) all-reduce(f32[8,128]{1,0:T(8,128)S(1)} %fusion.40, f32[8]{0:T(128)S(1)} %get-tuple-element.10), channel_id=1, replica_groups=mesh['gx'=16,'gy'=8] {'gx','gy'}, use_global_device_ids=true, to_apply=%region_1.2 | all-reduce | flops 1032 | bytes 8256 | tf_op jit(solution)/shard_map/psum | solution.py:70
  180.9 4.1 %copy.17 = f32[8,8,16,512]{3,2,1,0:T(8,128)} copy(f32[8,8,16,512]{3,0,2,1:T(8,128)} %get-tuple-element.11) | data formatting | bytes 4194304
  (24 shorter events, 6.1 us)
Async XLA Ops:
  5.9 12.9 %copy-start.1 = (f32[6,8,16,512]{3,2,1,0:T(8,128)S(1)}, f32[6,8,16,512]{3,2,1,0:T(8,128)}, u32[]{:S(2)}) copy-start(f32[6,8,16,512]{3,2,1,0:T(8,128)} %param.5) | copy-start | bytes 4718596
  6.0 6.1 %collective-permute-start = (f32[8,1,16,512]{3,0,2,1:T(8,128)S(1)}, f32[8,1,16,512]{3,0,2,1:T(8,128)S(1)}, u32[]{:S(2)}, u32[]{:S(2)}) collective-permute-start(f32[8,1,16,512]{3,0,2,1:T(8,128)S(1)} %get-tuple-element.25), channel_id=1, source_target_pairs={{0,8},{8,16},{16,24},{24,32},{32,40},{40,48},{48,56},{56,64},{64,7... | collective-permute-start | bytes 786440 | tf_op jit(solution)/shard_map/ppermute | solution.py:17
  8.7 6.1 %collective-permute-start.1 = (f32[8,1,16,512]{3,0,2,1:T(8,128)S(1)}, f32[8,1,16,512]{3,0,2,1:T(8,128)S(1)}, u32[]{:S(2)}, u32[]{:S(2)}) collective-permute-start(f32[8,1,16,512]{3,0,2,1:T(8,128)S(1)} %get-tuple-element.26), channel_id=1, source_target_pairs={{8,0},{16,8},{24,16},{32,24},{40,32},{48,40},{56,48},{64,56},{72,6... | collective-permute-start | bytes 786440 | tf_op jit(solution)/shard_map/ppermute | solution.py:19
  14.9 6.6 %copy-start = (f32[8,8,16,512]{3,2,1,0:T(8,128)S(1)}, f32[8,8,16,512]{3,2,1,0:T(8,128)}, u32[]{:S(2)}) copy-start(f32[8,8,16,512]{3,2,1,0:T(8,128)} %param.4) | copy-start | bytes 6291460
  14.9 6.6 %collective-permute-start.2 = (f32[8,10,1,512]{3,0,2,1:T(8,128)S(1)}, f32[8,10,1,512]{3,0,2,1:T(8,128)S(1)}, u32[]{:S(2)}, u32[]{:S(2)}) collective-permute-start(f32[8,10,1,512]{3,0,2,1:T(8,128)S(1)} %get-tuple-element.19), channel_id=1, source_target_pairs={{0,1},{1,2},{2,3},{3,4},{4,5},{5,6},{6,7},{7,0},{8,9},{9,10},{10,1... | collective-permute-start | bytes 491528 | tf_op jit(solution)/shard_map/ppermute | solution.py:17
  16.1 5.3 %collective-permute-start.3 = (f32[8,10,1,512]{3,0,2,1:T(8,128)S(1)}, f32[8,10,1,512]{3,0,2,1:T(8,128)S(1)}, u32[]{:S(2)}, u32[]{:S(2)}) collective-permute-start(f32[8,10,1,512]{3,0,2,1:T(8,128)S(1)} %get-tuple-element.20), channel_id=1, source_target_pairs={{1,0},{2,1},{3,2},{4,3},{5,4},{6,5},{7,6},{0,7},{9,8},{10,9},{11,1... | collective-permute-start | bytes 491528 | tf_op jit(solution)/shard_map/ppermute | solution.py:19
  27.1 4.8 %collective-permute-start.4 = (f32[8,1,16,512]{3,0,2,1:T(8,128)S(1)}, f32[8,1,16,512]{3,0,2,1:T(8,128)S(1)}, u32[]{:S(2)}, u32[]{:S(2)}) collective-permute-start(f32[8,1,16,512]{3,0,2,1:T(8,128)S(1)} %get-tuple-element.23), channel_id=1, source_target_pairs={{0,8},{8,16},{16,24},{24,32},{32,40},{40,48},{48,56},{56,64},{64,7... | collective-permute-start | bytes 786440 | tf_op jit(solution)/shard_map/ppermute | solution.py:17
  28.5 5.8 %collective-permute-start.5 = (f32[8,1,16,512]{3,0,2,1:T(8,128)S(1)}, f32[8,1,16,512]{3,0,2,1:T(8,128)S(1)}, u32[]{:S(2)}, u32[]{:S(2)}) collective-permute-start(f32[8,1,16,512]{3,0,2,1:T(8,128)S(1)} %get-tuple-element.24), channel_id=1, source_target_pairs={{8,0},{16,8},{24,16},{32,24},{40,32},{48,40},{56,48},{64,56},{72,6... | collective-permute-start | bytes 786440 | tf_op jit(solution)/shard_map/ppermute | solution.py:19
  34.3 7.7 %collective-permute-start.6 = (f32[8,10,1,512]{3,0,2,1:T(8,128)S(1)}, f32[8,10,1,512]{3,0,2,1:T(8,128)S(1)}, u32[]{:S(2)}, u32[]{:S(2)}) collective-permute-start(f32[8,10,1,512]{3,0,2,1:T(8,128)S(1)} %get-tuple-element.17), channel_id=1, source_target_pairs={{0,1},{1,2},{2,3},{3,4},{4,5},{5,6},{6,7},{7,0},{8,9},{9,10},{10,1... | collective-permute-start | bytes 491528 | tf_op jit(solution)/shard_map/ppermute | solution.py:17
  35.5 6.5 %collective-permute-start.7 = (f32[8,10,1,512]{3,0,2,1:T(8,128)S(1)}, f32[8,10,1,512]{3,0,2,1:T(8,128)S(1)}, u32[]{:S(2)}, u32[]{:S(2)}) collective-permute-start(f32[8,10,1,512]{3,0,2,1:T(8,128)S(1)} %get-tuple-element.18), channel_id=1, source_target_pairs={{1,0},{2,1},{3,2},{4,3},{5,4},{6,5},{7,6},{0,7},{9,8},{10,9},{11,1... | collective-permute-start | bytes 491528 | tf_op jit(solution)/shard_map/ppermute | solution.py:19
  47.8 6.6 %collective-permute-start.8 = (f32[8,1,16,512]{3,0,2,1:T(8,128)S(1)}, f32[8,1,16,512]{3,0,2,1:T(8,128)S(1)}, u32[]{:S(2)}, u32[]{:S(2)}) collective-permute-start(f32[8,1,16,512]{3,0,2,1:T(8,128)S(1)} %get-tuple-element.21), channel_id=1, source_target_pairs={{0,8},{8,16},{16,24},{24,32},{32,40},{40,48},{48,56},{56,64},{64,7... | collective-permute-start | bytes 786440 | tf_op jit(solution)/shard_map/ppermute | solution.py:17
  48.5 6.1 %collective-permute-start.9 = (f32[8,1,16,512]{3,0,2,1:T(8,128)S(1)}, f32[8,1,16,512]{3,0,2,1:T(8,128)S(1)}, u32[]{:S(2)}, u32[]{:S(2)}) collective-permute-start(f32[8,1,16,512]{3,0,2,1:T(8,128)S(1)} %get-tuple-element.22), channel_id=1, source_target_pairs={{8,0},{16,8},{24,16},{32,24},{40,32},{48,40},{56,48},{64,56},{72,6... | collective-permute-start | bytes 786440 | tf_op jit(solution)/shard_map/ppermute | solution.py:19
  54.7 7.0 %collective-permute-start.10 = (f32[8,10,1,512]{3,0,2,1:T(8,128)S(1)}, f32[8,10,1,512]{3,0,2,1:T(8,128)S(1)}, u32[]{:S(2)}, u32[]{:S(2)}) collective-permute-start(f32[8,10,1,512]{3,0,2,1:T(8,128)S(1)} %get-tuple-element.15), channel_id=1, source_target_pairs={{0,1},{1,2},{2,3},{3,4},{4,5},{5,6},{6,7},{7,0},{8,9},{9,10},{10,1... | collective-permute-start | bytes 491528 | tf_op jit(solution)/shard_map/ppermute | solution.py:17
  56.5 5.2 %collective-permute-start.11 = (f32[8,10,1,512]{3,0,2,1:T(8,128)S(1)}, f32[8,10,1,512]{3,0,2,1:T(8,128)S(1)}, u32[]{:S(2)}, u32[]{:S(2)}) collective-permute-start(f32[8,10,1,512]{3,0,2,1:T(8,128)S(1)} %get-tuple-element.16), channel_id=1, source_target_pairs={{1,0},{2,1},{3,2},{4,3},{5,4},{6,5},{7,6},{0,7},{9,8},{10,9},{11,1... | collective-permute-start | bytes 491528 | tf_op jit(solution)/shard_map/ppermute | solution.py:19
where the time goes:
time: 185 us
  blocking collectives  79.7 us (43%)
  matrix products  29.1 us (16%)
  other arithmetic  24.6 us (13%)
  starting transfers between devices  24.6 us (13%)
  waiting for transfers between devices  19.4 us (10%)
  local copies, waits for them, and re-layouts  6.95 us (4%)
    psum x1, blocking collectives, local(): gram, norm_total = lax.psum((gram_part, norm_part), ('gx', 'gy'))  79.7 us
    dot_general x1, matrix products, local(): lax.dot_general(flat, observer.reshape(QCOLS, -1), (((1,), (1,)), ((), ()...  29.1 us
    ppermute x6, starting transfers between devices, padded_2(): lax.ppermute(head, axis, [((i + 1) % count, i) for i in range(count)])  15.4 us
    ppermute x6, waiting for transfers between devices, padded_2(): lax.ppermute(tail, axis, [(i, (i + 1) % count) for i in range(count)])  14 us
    ppermute x6, starting transfers between devices, padded_2(): lax.ppermute(tail, axis, [(i, (i + 1) % count) for i in range(count)])  9.16 us
    reduce_sum x1, other arithmetic, local(): norm_part = jnp.sum(new_resid * new_resid, axis=(1, 2, 3))  7.05 us
    unnamed x6, local copies, waits for them, and re-layouts  6.67 us
    add x1, other arithmetic, chebyshev(): third = start + omega_two * (jacobi(second) - start)  5.77 us
  transfers between devices with their start and end apart: 12, of which 9 were waited for; matrix products, arithmetic and copies ran while one was open for 0% of the time, Pallas kernels for 0%

commit v1 on v0

v1 whole, which is shorter than its diff:
```python
import jax
import jax.numpy as jnp
from jax import lax
from jax.experimental import pallas as pl
from jax.experimental.pallas import tpu as pltpu
from jax.sharding import Mesh, PartitionSpec as P

COLS = 8
QCOLS = 128
LX = 8
LY = 16
CELLS = LX * LY
NZ = 512
ZT = NZ // 128
STEP = CELLS * ZT
F32 = jnp.float32
BF16 = jnp.bfloat16

GX = ("zh", "y", "core")
GY = ("zl", "x")
CHIPS = ("zh", "y", "zl", "x")

VM = pl.BlockSpec(memory_space=pltpu.VMEM)
HB = pl.BlockSpec(memory_space=pltpu.HBM)
SM = pl.BlockSpec(memory_space=pltpu.SMEM)

FIELD = (CELLS, COLS, NZ)
XFACE = (LY, COLS, NZ)
YFACE = (LX, COLS, NZ)


def sds(shape, dtype=F32):
    return jax.ShapeDtypeStruct(shape, dtype)


def stored(block):
    n = block.shape[0]
    return block.reshape(n, LX, LY // 8, 8, ZT, 128).transpose(0, 1, 2, 4, 3, 5).reshape(n * STEP, 128)


def unstored(rows):
    n = rows.shape[0] // STEP
    return rows.reshape(n, LX, LY // 8, ZT, 8, 128).transpose(0, 1, 2, 4, 3, 5).reshape(n, LX, LY, NZ)


def base(r):
    return (r // 8) * 32 + lax.rem(r, 8)


def spot(r):
    return r if isinstance(r, tuple) else (r // 8, lax.rem(r, 8))


def coef(c_ref, k, r):
    t, j = spot(r)
    at = k * STEP + t * 32 + j
    return jnp.concatenate([c_ref[pl.ds(at + zt * 8, COLS, stride=0), :] for zt in range(ZT)], axis=1)


def columns(r_ref, r):
    t, j = spot(r)
    at = t * 32 + j
    return jnp.concatenate([r_ref[pl.ds(at + zt * 8, COLS, stride=STEP), :] for zt in range(ZT)], axis=1)


def put_columns(o_ref, r, v):
    t, j = spot(r)
    at = t * 32 + j
    for zt in range(ZT):
        o_ref[pl.ds(at + zt * 8, COLS, stride=STEP), :] = v[:, zt * 128 : zt * 128 + 128]


def wide(v):
    return jnp.concatenate([v] * ZT, axis=1)


def x_row(high, i):
    return jnp.where(high, CELLS - LY, 0) + i


def y_row(high, i):
    return jnp.where(high, LY - 1, 0) + LY * i


def face_sides():
    even_x = lax.axis_index("core") == 0
    even_y = lax.rem(lax.axis_index("x"), 2) == 0
    return jnp.logical_not(even_x), jnp.logical_not(even_y), even_y, even_x


def first_kernel(shift_ref, r_hbm, c_hbm, sb, sd, sc, sa, prm, rs, cs, sem):
    get_c = pltpu.make_async_copy(c_hbm, cs, sem.at[0])
    get_r = pltpu.make_async_copy(r_hbm, rs, sem.at[1])
    get_c.start()
    get_r.start()
    row = lax.broadcasted_iota(jnp.int32, (COLS, 128), 0)
    index = jnp.zeros((COLS, 128), F32)
    for c in range(COLS):
        index = jnp.where(row == c, shift_ref[c].astype(F32), index)
    sigma = 0.2 * jnp.exp(jnp.log(jnp.full((COLS, 128), 40.0, F32)) * index / 15.0)
    radius = 12.0 / (12.0 + sigma)
    omega_two = 1.0 / (1.0 - radius * radius / 2.0)
    omega_three = 1.0 / (1.0 - radius * radius * omega_two / 4.0)
    prm[0] = sigma
    prm[1] = omega_two
    prm[2] = omega_three
    prm[3] = jnp.sqrt(2.0 * sigma)
    prm[4] = 2.0 * sigma
    fb, fd, fc, fa = face_sides()
    sigma = wide(sigma)
    get_c.wait()
    get_r.wait()

    def start_of(r):
        d = coef(cs, 0, r)
        for k in range(1, 6):
            d = d + coef(cs, k, r)
        return columns(rs, r) / (d + sigma)

    tb, ta = jnp.where(fb, CELLS // 8 - 2, 0), jnp.where(fa, CELLS // 8 - 2, 0)
    for j in range(8):
        for half in range(2):
            sb[half * 8 + j] = start_of((tb + half, j))
            sa[half * 8 + j] = start_of((ta + half, j))

    def ys(i, _):
        sd[i] = start_of(y_row(fd, i))
        sc[i] = start_of(y_row(fc, i))
        return 0

    lax.fori_loop(0, LX, ys, 0, unroll=4)


def spread(f_ref, cz, t, j):
    r = 8 * t + j
    v = f_ref[r]
    below = jnp.maximum(r - 1, 0) if j == 0 else r - 1
    above = jnp.minimum(r + 1, CELLS - 1) if j == 7 else r + 1
    total = coef(cz, 4, (t, j)) * pltpu.roll(v, 1, 1)
    total += coef(cz, 5, (t, j)) * pltpu.roll(v, NZ - 1, 1)
    total += coef(cz, 0, (t, j)) * f_ref[8 * jnp.maximum(t - 2, 0) + j]
    total += coef(cz, 1, (t, j)) * f_ref[8 * jnp.minimum(t + 2, CELLS // 8 - 1) + j]
    total += coef(cz, 2, (t, j)) * f_ref[below]
    total += coef(cz, 3, (t, j)) * f_ref[above]
    return total


def second_kernel(rs, cs, prm, o_hbm, start, rdiag, resid, cz, part, ov, sem):
    load = pltpu.make_async_copy(o_hbm, ov, sem)
    load.start()
    sigma = wide(prm[0])
    row = lax.broadcasted_iota(jnp.int32, (64, 128), 0)
    lane = lax.broadcasted_iota(jnp.int32, (64, 128), 1)
    in32, in8 = lax.rem(row, 32), lax.rem(row, 8)
    outside = (
        None,
        None,
        jnp.logical_and(row < 32, in8 == 0),
        jnp.logical_and(row >= 32, in8 == 7),
        jnp.logical_and(in32 < 8, lane == 0),
        jnp.logical_and(in32 >= 24, lane == 127),
    )
    for k in range(6):
        for x in range(LX):
            rows = pl.ds(k * STEP + x * 64, 64)
            if (k, x) in ((0, 0), (1, LX - 1)):
                cz[rows, :] = jnp.zeros((64, 128), F32)
            elif k < 2:
                cz[rows, :] = cs[rows, :]
            else:
                cz[rows, :] = jnp.where(outside[k], 0.0, cs[rows, :])

    def begin(t, _):
        for j in range(8):
            d = coef(cs, 0, (t, j))
            for k in range(1, 6):
                d = d + coef(cs, k, (t, j))
            recip = 1.0 / (d + sigma)
            res = columns(rs, (t, j))
            resid[8 * t + j] = res
            rdiag[8 * t + j] = recip
            start[8 * t + j] = res * recip
        return 0

    lax.fori_loop(0, CELLS // 8, begin, 0)

    def sweep(t, _):
        for j in range(8):
            r = 8 * t + j
            part[r] = (resid[r] + spread(start, cz, t, j)) * rdiag[r]
        return 0

    lax.fori_loop(0, CELLS // 8, sweep, 0)
    load.wait()


def third_kernel(field, before, resid, rdiag, cz, prm, part):
    omega = wide(prm[1])

    def sweep(t, _):
        for j in range(8):
            r = 8 * t + j
            s = before[r]
            part[r] = s + omega * ((resid[r] + spread(field, cz, t, j)) * rdiag[r] - s)
        return 0

    lax.fori_loop(0, CELLS // 8, sweep, 0)


def fourth_kernel(field, before, resid, rdiag, cz, prm, part, fscr, nscr, low, total):
    omega, root, twice = wide(prm[2]), wide(prm[3]), wide(prm[4])
    total[...] = jnp.zeros((COLS, NZ), F32)

    def sweep(t, _):
        inner = jnp.where(jnp.logical_and(t >= 2, t < CELLS // 8 - 2), 1.0, 0.0)
        odd = lax.rem(t, 2).astype(F32)
        added = None
        for j0 in range(0, 8, 2):
            pair = []
            for j in (j0, j0 + 1):
                r = 8 * t + j
                s = before[r]
                s = s + omega * ((resid[r] + spread(field, cz, t, j)) * rdiag[r] - s)
                part[r] = s
                f = root * s
                n = resid[r] - twice * s
                put_columns(fscr, (t, j), f)
                put_columns(nscr, (t, j), n)
                n = n * n
                if j == 0:
                    n = n * odd
                if j == 7:
                    n = n * (1.0 - odd)
                added = n if added is None else added + n
                pair.append(f)
            low[pl.ds(pl.multiple_of(64 * t + 8 * j0, 16), 16), :] = jnp.concatenate(pair, axis=0).astype(BF16)
        total[...] += inner * added
        return 0

    lax.fori_loop(0, CELLS // 8, sweep, 0)


def fix_faces(field, rdiag, cs, halos, scale):
    fb, fd, fc, fa = face_sides()
    rb, rd, rc, ra = halos

    def add(r, k, halo):
        v = coef(cs, k, r) * halo
        t, j = spot(r)
        v = v * rdiag[8 * t + j]
        if scale is not None:
            v = v * scale
        field[8 * t + j] += v

    tb, ta = jnp.where(fb, CELLS // 8 - 2, 0), jnp.where(fa, CELLS // 8 - 2, 0)
    kb, kd, kc, ka = jnp.where(fb, 1, 0), jnp.where(fd, 3, 2), jnp.where(fc, 3, 2), jnp.where(fa, 1, 0)
    for half in range(2):
        for j in range(8):
            add((tb + half, j), kb, rb[half * 8 + j])
            add((ta + half, j), ka, ra[half * 8 + j])

    def ys(i, _):
        add(y_row(fd, i), kd, rd[i])
        add(y_row(fc, i), kc, rc[i])
        return 0

    lax.fori_loop(0, LX, ys, 0, unroll=4)


def fix_kernel(which, old, rdiag, cs, prm, rb, rd, rc, ra, field, sb, sd, sc, sa):
    del old
    fix_faces(field, rdiag, cs, (rb, rd, rc, ra), wide(prm[which]) if which else None)
    fb, fd, fc, fa = face_sides()
    sb[...] = field[pl.ds(x_row(fb, 0), LY)]
    sa[...] = field[pl.ds(x_row(fa, 0), LY)]
    for i in range(LX):
        sd[i] = field[y_row(fd, i)]
        sc[i] = field[y_row(fc, i)]


def last_kernel(
    old, old_f, old_n, old_low, inner, rdiag, resid, cs, prm, rb, rd, rc, ra, ov,
    field, fscr, nscr, low, fac_hbm, new_hbm, msg, gq, sem,
):
    del old, old_f, old_n, old_low
    fix_faces(field, rdiag, cs, (rb, rd, rc, ra), wide(prm[2]))
    root, twice = wide(prm[3]), wide(prm[4])

    def finish(t, j0, counted):
        pair, added = [], None
        for j in (j0, j0 + 1):
            s = field[8 * t + j]
            f = root * s
            n = resid[8 * t + j] - twice * s
            put_columns(fscr, (t, j), f)
            put_columns(nscr, (t, j), n)
            if j in counted:
                added = n * n if added is None else added + n * n
            pair.append(f)
        low[pl.ds(pl.multiple_of(64 * t + 8 * j0, 16), 16), :] = jnp.concatenate(pair, axis=0).astype(BF16)
        return added

    total = inner[...]
    for t in (0, 1, CELLS // 8 - 2, CELLS // 8 - 1):
        for j0 in range(0, 8, 2):
            total = total + finish(t, j0, (j0, j0 + 1))

    def sides(x, total):
        return total + finish(2 * x, 0, (0,)) + finish(2 * x + 1, 6, (7,))

    total = lax.fori_loop(1, LX - 1, sides, total, unroll=2)
    put_f = pltpu.make_async_copy(fscr, fac_hbm, sem.at[0])
    put_n = pltpu.make_async_copy(nscr, new_hbm, sem.at[1])
    put_f.start()
    put_n.start()
    block = 64

    def gram(q, _):
        q0 = q * block
        p = None
        for x in range(LX):
            o = ov[pl.ds(q0, block), x].reshape(block * LY, NZ)
            w = low[x * 128 : x * 128 + 128, :]
            d = lax.dot_general(o, w, (((1,), (1,)), ((), ())), preferred_element_type=F32)
            p = d if p is None else p + d
        p = p.reshape(block, LY, 128)
        ysub = lax.broadcasted_iota(jnp.int32, (LY, 128), 0)
        ylane = lax.broadcasted_iota(jnp.int32, (LY, 128), 1) // COLS
        g = jnp.sum(jnp.where((ysub == ylane)[None], p, 0.0), axis=1)
        for shift in (64, 32, 16, 8):
            g = g + pltpu.roll(g, shift, 1)
        gq[pl.ds(pl.multiple_of(q0, block), block), :] = g
        return 0

    lax.fori_loop(0, QCOLS // block, gram, 0)
    g = jnp.transpose(gq[...])
    for c in range(COLS):
        msg[0:1, c * 128 : c * 128 + 128] = g[c : c + 1, :]
    squares = jnp.broadcast_to(jnp.sum(total, axis=1, keepdims=True), (COLS, 128))
    row = lax.broadcasted_iota(jnp.int32, (COLS, 128), 0)
    lane = lax.broadcasted_iota(jnp.int32, (COLS, 128), 1)
    msg[0:1, COLS * 128 :] = jnp.sum(jnp.where(row == lane, squares, 0.0), axis=0, keepdims=True)
    put_f.wait()
    put_n.wait()


def sum_kernel(parts, gram, norms):
    total = jnp.sum(parts[...], axis=0)
    for c in range(COLS):
        gram[c : c + 1, :] = total[:, c * 128 : c * 128 + 128]
    norms[...] = total[:, COLS * 128 :] / (CELLS * NZ * 128)


LIMIT = pltpu.CompilerParams(vmem_limit_bytes=8 << 20)
SENDS = (sds(XFACE), sds(YFACE), sds(YFACE), sds(XFACE))
ROWS = sds((COLS * STEP, 128))
COEFS = sds((6 * STEP, 128))


def in_hbm(x):
    return pltpu.with_memory_space_constraint(x, pltpu.HBM)


def pairs(n, first):
    out = []
    for i in range(first, n, 2):
        out += [(i, (i + 1) % n), ((i + 1) % n, i)]
    return out


def exchange(sends):
    sb, sd, sc, sa = sends
    rb = lax.ppermute(sb, GX, pairs(16, 1))
    rd = lax.ppermute(sd, GY, pairs(8, 1))
    rc = lax.ppermute(sc, GY, pairs(8, 0))
    ra = lax.ppermute(sa, GX, pairs(16, 0))
    return rb, rd, rc, ra


def local(resid_factor, coefficients, observer, shift_index):
    *sends, prm, rs, cs = pl.pallas_call(
        first_kernel, out_shape=(*SENDS, sds((5, COLS, 128)), ROWS, COEFS), in_specs=[SM, HB, HB], out_specs=(VM,) * 7,
        scratch_shapes=[pltpu.SemaphoreType.DMA((2,))], compiler_params=LIMIT, name="first",
    )(shift_index, in_hbm(stored(resid_factor)), in_hbm(stored(coefficients)))
    halos = exchange(sends)
    start, rdiag, resid, cz, part, seen = pl.pallas_call(
        second_kernel,
        out_shape=(sds(FIELD), sds(FIELD), sds(FIELD), COEFS, sds(FIELD), sds(observer.shape, BF16)),
        in_specs=[VM, VM, VM, HB], out_specs=(VM,) * 6, scratch_shapes=[pltpu.SemaphoreType.DMA],
        compiler_params=LIMIT, name="bulk_second",
    )(rs, cs, prm, in_hbm(observer))

    def fixed(which, part, halos):
        return pl.pallas_call(
            lambda *refs: fix_kernel(which, *refs), out_shape=(sds(FIELD), *SENDS), in_specs=[VM] * 8, out_specs=(VM,) * 5,
            input_output_aliases={0: 0}, compiler_params=LIMIT, name=f"fix_{which}",
        )(part, rdiag, cs, prm, *halos)

    second, *sends = fixed(0, part, halos)
    halos = exchange(sends)
    part = pl.pallas_call(
        third_kernel, out_shape=sds(FIELD), in_specs=[VM] * 6, out_specs=VM, compiler_params=LIMIT, name="bulk_third",
    )(second, start, resid, rdiag, cz, prm)
    third, *sends = fixed(1, part, halos)
    halos = exchange(sends)
    low = sds((COLS * CELLS, NZ), BF16)
    part, fscr, nscr, low_part, inner = pl.pallas_call(
        fourth_kernel, out_shape=(sds(FIELD), ROWS, ROWS, low, sds((COLS, NZ))), in_specs=[VM] * 6, out_specs=(VM,) * 5,
        compiler_params=LIMIT, name="bulk_fourth",
    )(third, second, resid, rdiag, cz, prm)
    *_, fac, new, msg = pl.pallas_call(
        last_kernel,
        out_shape=(sds(FIELD), ROWS, ROWS, low, ROWS, ROWS, sds((1, 9 * 128))),
        in_specs=[VM] * 14, out_specs=(VM, VM, VM, VM, HB, HB, VM), input_output_aliases={0: 0, 1: 1, 2: 2, 3: 3},
        scratch_shapes=[pltpu.VMEM((QCOLS, 128), F32), pltpu.SemaphoreType.DMA((2,))],
        compiler_params=LIMIT, name="last",
    )(part, fscr, nscr, low_part, inner, rdiag, resid, cs, prm, *halos, seen)
    msg = msg + lax.ppermute(msg, "core", [(0, 1), (1, 0)])
    gathered = lax.all_to_all(jnp.broadcast_to(msg, (64,) + msg.shape), CHIPS, 0, 0)
    gram, norms = pl.pallas_call(
        sum_kernel, out_shape=(sds((COLS, 128)), sds((1, 128))), in_specs=[VM], out_specs=(VM, VM), name="total",
    )(gathered)
    return unstored(fac), unstored(new), gram, norms[0, :COLS]


def solution(mesh):
    shape = (2, 4, 2, 2, 4)
    fine = Mesh(mesh.devices.reshape(shape), ("zh", "y", "core", "zl", "x"))
    placed = P(None, GX, GY, None)
    return jax.shard_map(
        local, mesh=fine, in_specs=(placed, placed, placed, P()), out_specs=(placed, placed, P(), P()), check_vma=False
    )
```

time: 185 us -> 73.9 us (0.40)
  blocking collectives: 79.7 us -> 17.7 us
  matrix products: 29.1 us -> 0 us
  Pallas kernels: 0 us -> 26.6 us
  other arithmetic: 24.6 us -> 0.02 us
  waiting for transfers between devices: 19.4 us -> 2.64 us
  local copies, waits for them, and re-layouts: 6.95 us -> 1.97 us
    psum x1 -> x0, blocking collectives: 79.7 us -> none  [local(): gram, norm_total = lax.psum((gram_part, norm_part), ('gx', 'gy'))]
    dot_general x1 -> x0, matrix products: 29.1 us -> none  [local(): lax.dot_general(flat, observer.reshape(QCOLS, -1), (((1,), (1,)), ((), ()...]
    pallas_call x0 -> x8, Pallas kernels: none -> 26.6 us  [the longest x1 6.73 us: local(): pl.pallas_call(last_kernel, out_shape=(sds(FIELD), ROWS, ROWS, low, ROWS,...]
    all_to_all x0 -> x1, blocking collectives: none -> 17.7 us  [local(): lax.all_to_all(jnp.broadcast_to(msg, (64,) + msg.shape), CHIPS, 0, 0)]
    ppermute x12 -> x13, waiting for transfers between devices: 19.4 us -> 2.64 us  [the longest x3 1.24 us: exchange(): rd = lax.ppermute(sd, GY, pairs(8, 1))]
    div x4 -> x0, other arithmetic: 9.1 us -> none  [the longest x1 5.54 us: jacobi(): return (resid_factor + spread(face_padded(field), coefficients)) / diagonal]
    reduce_sum x2 -> x0, other arithmetic: 8.64 us -> none  [the longest x1 7.05 us: local(): norm_part = jnp.sum(new_resid * new_resid, axis=(1, 2, 3))]
    unnamed x6 -> x2, local copies, waits for them, and re-layouts: 6.67 us -> 0.65 us
  transfers between devices with their start and end apart: 12 -> 13, of which waited for: 9 -> 3; matrix products, arithmetic and copies ran while one was open for 0% -> 0% of each run, Pallas kernels for 0% -> 19%
where the time goes in v1:
time: 73.9 us; the launch traced here: 73.6 us
  Pallas kernels  26.6 us (36%)
  starting transfers between devices  23.9 us (32%)
  blocking collectives  17.7 us (24%)
  waiting for transfers between devices  2.64 us (4%)
  local copies, waits for them, and re-layouts  1.97 us (3%)
  between operations  0.79 us (1%)
    all_to_all x1, blocking collectives, local(): lax.all_to_all(jnp.broadcast_to(msg, (64,) + msg.shape), CHIPS, 0, 0)  17.7 us
    ppermute x3, starting transfers between devices, exchange(): ra = lax.ppermute(sa, GX, pairs(16, 0))  11.9 us
    ppermute x3, starting transfers between devices, exchange(): rd = lax.ppermute(sd, GY, pairs(8, 1))  8.42 us
    pallas_call x1, Pallas kernels, local(): pl.pallas_call(last_kernel, out_shape=(sds(FIELD), ROWS, ROWS, low, ROWS,...  6.73 us
    pallas_call x1, Pallas kernels, local(): pl.pallas_call(second_kernel, out_shape=(sds(FIELD), sds(FIELD), sds(FIEL...  5.78 us
    pallas_call x1, Pallas kernels, local(): pl.pallas_call(fourth_kernel, out_shape=(sds(FIELD), ROWS, ROWS, low, sds...  5.29 us
    pallas_call x1, Pallas kernels, local(): pl.pallas_call(first_kernel, out_shape=(*SENDS, sds((5, COLS, 128)), ROWS...  3.35 us
    pallas_call x1, Pallas kernels, local(): pl.pallas_call(third_kernel, out_shape=sds(FIELD), in_specs=[VM] * 6, out...  2.97 us
  transfers between devices with their start and end apart: 13, of which 3 were waited for; matrix products, arithmetic and copies ran while one was open for 0% of the time, Pallas kernels for 19%

profile of v1, /device:TPU:1, one launch (start us, length us, event | category | flops | bytes accessed | tf_op | source)
XLA Modules:
  0.0 73.6 jit_solution(14995234899930540601)
XLA Ops:
  0.6 0.6 copy-done
  1.3 3.4 %first.1 = (f32[16,8,512]{2,1,0:T(8,128)S(1)}, f32[8,8,512]{2,1,0:T(8,128)S(1)}, f32[8,8,512]{2,1,0:T(8,128)S(1)}, f32[16,8,512]{2,1,0:T(8,128)S(1)}, f32[5,8,12...) custom-call(s32[8]{0:T(128)S(1)} %copy-done, f32[4096,128]{1,0:T(8,128)} %bitcast.22, ...), custom_call_target="tpu_custom_call" | custom-call | tf_op jit(solution)/shard_map/first/pallas_call | solution.py:381
  4.6 2.8 %collective-permute-start = (f32[16,8,512]{2,1,0:T(8,128)S(1)}, f32[16,8,512]{2,1,0:T(8,128)S(1)}, u32[]{:S(2)}, u32[]{:S(2)}) collective-permute-start(f32[16,8,512]{2,1,0:T(8,128)S(1)} %get-tuple-element.42), channel_id=1, source_target_pairs={{8,16},{16,8},{24,32},{32,24},{40,48},{48,40},{56,64},{64,56},{72,... | collective-permute-start | bytes 786440 | tf_op jit(solution)/shard_map/ppermute | solution.py:373
  7.4 4.6 %collective-permute-start.3 = (f32[16,8,512]{2,1,0:T(8,128)S(1)}, f32[16,8,512]{2,1,0:T(8,128)S(1)}, u32[]{:S(2)}, u32[]{:S(2)}) collective-permute-start(f32[16,8,512]{2,1,0:T(8,128)S(1)} %get-tuple-element.45), channel_id=1, source_target_pairs={{0,8},{8,0},{16,24},{24,16},{32,40},{40,32},{48,56},{56,48},{64,72... | collective-permute-start | bytes 786440 | tf_op jit(solution)/shard_map/ppermute | solution.py:376
  12.0 2.9 %collective-permute-start.1 = (f32[8,8,512]{2,1,0:T(8,128)S(1)}, f32[8,8,512]{2,1,0:T(8,128)S(1)}, u32[]{:S(2)}, u32[]{:S(2)}) collective-permute-start(f32[8,8,512]{2,1,0:T(8,128)S(1)} %get-tuple-element.43), channel_id=1, source_target_pairs={{1,2},{2,1},{3,4},{4,3},{5,6},{6,5},{7,0},{0,7},{9,10},{10,9},{11,... | collective-permute-start | bytes 393224 | tf_op jit(solution)/shard_map/ppermute | solution.py:374
  14.9 5.8 %bulk_second.1 = (f32[128,8,512]{2,1,0:T(8,128)S(1)}, f32[128,8,512]{2,1,0:T(8,128)S(1)}, f32[128,8,512]{2,1,0:T(8,128)S(1)}, f32[3072,128]{1,0:T(8,128)S(1)}, f...) custom-call(f32[4096,128]{1,0:T(8,128)S(1)} %get-tuple-element.37.rs, ...), custom_call_target="tpu_custom_call" | custom-call | tf_op jit(solution)/shard_map/bulk_second/pallas_call | solution.py:386
  20.8 0.3 fix_0.1
  21.2 3.0 %collective-permute-start.7 = (f32[16,8,512]{2,1,0:T(8,128)S(1)}, f32[16,8,512]{2,1,0:T(8,128)S(1)}, u32[]{:S(2)}, u32[]{:S(2)}) collective-permute-start(f32[16,8,512]{2,1,0:T(8,128)S(1)} %get-tuple-element.53), channel_id=1, source_target_pairs={{0,8},{8,0},{16,24},{24,16},{32,40},{40,32},{48,56},{56,48},{64,72... | collective-permute-start | bytes 786440 | tf_op jit(solution)/shard_map/ppermute | solution.py:376
  24.2 2.9 %collective-permute-start.5 = (f32[8,8,512]{2,1,0:T(8,128)S(1)}, f32[8,8,512]{2,1,0:T(8,128)S(1)}, u32[]{:S(2)}, u32[]{:S(2)}) collective-permute-start(f32[8,8,512]{2,1,0:T(8,128)S(1)} %get-tuple-element.51), channel_id=1, source_target_pairs={{1,2},{2,1},{3,4},{4,3},{5,6},{6,5},{7,0},{0,7},{9,10},{10,9},{11,... | collective-permute-start | bytes 393224 | tf_op jit(solution)/shard_map/ppermute | solution.py:374
  27.2 3.0 %bulk_third.1.refs_0_ = f32[128,8,512]{2,1,0:T(8,128)S(1)} custom-call(f32[128,8,512]{2,1,0:T(8,128)S(1)} %get-tuple-element.46.field.before, f32[128,8,512]{2,1,0:T(8,128)S(1)} %get-tuple-element.47.before, f32[128,8,512]{2,1,0:T(8,128)S(1)} %get-tuple-element.48.resid, f32[128,8,512]{2,1,0:T(8,128)S(1)} %get-tuple-element.41.refs_1_.rdiag, ...), custom_call_target="tpu_custom_call" | custom-call | tf_op jit(solution)/shard_map/bulk_third/pallas_call | solution.py:401
  30.2 1.2 %collective-permute-done.5.refs_5_ = f32[8,8,512]{2,1,0:T(8,128)S(1)} collective-permute-done((f32[8,8,512]{2,1,0:T(8,128)S(1)}, f32[8,8,512]{2,1,0:T(8,128)S(1)}, u32[]{:S(2)}, u32[]{:S(2)}) %collective-permute-start.5) | collective-permute-done | bytes 131104 | tf_op jit(solution)/shard_map/ppermute | solution.py:374
  31.4 0.6 collective-permute-done.6.refs_6_
  32.0 0.3 fix_1.1
  32.3 0.1 collective-permute-start.8
  32.4 4.3 %collective-permute-start.11 = (f32[16,8,512]{2,1,0:T(8,128)S(1)}, f32[16,8,512]{2,1,0:T(8,128)S(1)}, u32[]{:S(2)}, u32[]{:S(2)}) collective-permute-start(f32[16,8,512]{2,1,0:T(8,128)S(1)} %get-tuple-element.63), channel_id=1, source_target_pairs={{0,8},{8,0},{16,24},{24,16},{32,40},{40,32},{48,56},{56,48},{64,72... | collective-permute-start | bytes 786440 | tf_op jit(solution)/shard_map/ppermute | solution.py:376
  36.7 2.5 %collective-permute-start.9 = (f32[8,8,512]{2,1,0:T(8,128)S(1)}, f32[8,8,512]{2,1,0:T(8,128)S(1)}, u32[]{:S(2)}, u32[]{:S(2)}) collective-permute-start(f32[8,8,512]{2,1,0:T(8,128)S(1)} %get-tuple-element.61), channel_id=1, source_target_pairs={{1,2},{2,1},{3,4},{4,3},{5,6},{6,5},{7,0},{0,7},{9,10},{10,9},{11,... | collective-permute-start | bytes 393224 | tf_op jit(solution)/shard_map/ppermute | solution.py:374
  39.3 5.3 %bulk_fourth.1 = (f32[128,8,512]{2,1,0:T(8,128)S(1)}, f32[4096,128]{1,0:T(8,128)S(1)}, f32[4096,128]{1,0:T(8,128)S(1)}, bf16[1024,512]{1,0:T(8,128)(2,1)S(1)}, f32[8,512]{1,0:T(8,128)S(1)}) custom-call(f32[128,8,512]{2,1,0:T(8,128)S(1)} %get-tuple-element.54.field, f32[128,8,512]{2,1,0:T(8,128)S(1)} %get-tuple-element.46.field.before, ...), custom_call_target="tpu_custom_call" | custom-call | tf_op jit(solution)/shard_map/bulk_fourth/pallas_call | solution.py:407
  44.6 6.7 %last.1 = (f32[128,8,512]{2,1,0:T(8,128)S(1)}, f32[4096,128]{1,0:T(8,128)S(1)}, f32[4096,128]{1,0:T(8,128)S(1)}, bf16[1024,512]{1,0:T(8,128)(2,1)S(1)}, f32[4096...) custom-call(f32[128,8,512]{2,1,0:T(8,128)S(1)} %get-tuple-element.55, ...), custom_call_target="tpu_custom_call", output_to_operand_aliasing={{0}: (0, {}), {1}: (1, {}), {2}: (2, {}), {3}: (3, {})} | custom-call | tf_op jit(solution)/shard_map/last/pallas_call | solution.py:411
  51.3 0.6 collective-permute-start.12
  52.0 0.8 %collective-permute-done.12 = f32[1,1152]{1,0:T(1,128)S(1)} collective-permute-done((f32[1,1152]{1,0:T(1,128)S(1)}, f32[1,1152]{1,0:T(1,128)S(1)}, u32[]{:S(2)}, u32[]{:S(2)}) %collective-permute-start.12) | collective-permute-done | bytes 4640 | tf_op jit(solution)/shard_map/ppermute | solution.py:418
  52.8 0.2 broadcast_in_dim.3
  53.0 17.7 %all_to_all.5.parts = f32[64,1,1152]{2,1,0:T(1,128)} all-to-all(f32[64,1,1152]{2,1,0:T(1,128)S(1)} %broadcast_in_dim.3), channel_id=1, replica_groups=mesh['zh'=2,'y'=4,'core'=2,'zl'=2,'x'=4] {'zh','y','zl','x'}, dimensions={0} | all-to-all | bytes 589824 | tf_op jit(solution)/shard_map/all_to_all | solution.py:419
  70.7 1.8 %total.1 = (f32[8,128]{1,0:T(8,128)}, f32[1,128]{1,0:T(1,128)}) custom-call(f32[64,1,1152]{2,1,0:T(1,128)} %all_to_all.5.parts), custom_call_target="tpu_custom_call" | custom-call | tf_op jit(solution)/shard_map/total/pallas_call | solution.py:420
  72.4 1.2 %slice_bitcast_fusion = f32[8]{0:T(128)} fusion(f32[1,128]{1,0:T(1,128)} %get-tuple-element.69), kind=kLoop, calls=%fused_computation.1 | loop fusion | bytes 64 | tf_op jit(solution)/shard_map/squeeze | solution.py:423
  (16 shorter events, 0.1 us)
Async XLA Ops:
  0.6 0.7 copy-start
  4.6 16.1 %collective-permute-start = (f32[16,8,512]{2,1,0:T(8,128)S(1)}, f32[16,8,512]{2,1,0:T(8,128)S(1)}, u32[]{:S(2)}, u32[]{:S(2)}) collective-permute-start(f32[16,8,512]{2,1,0:T(8,128)S(1)} %get-tuple-element.42), channel_id=1, source_target_pairs={{8,16},{16,8},{24,32},{32,24},{40,48},{48,40},{56,64},{64,56},{72,... | collective-permute-start | bytes 786440 | tf_op jit(solution)/shard_map/ppermute | solution.py:373
  7.4 13.3 %collective-permute-start.3 = (f32[16,8,512]{2,1,0:T(8,128)S(1)}, f32[16,8,512]{2,1,0:T(8,128)S(1)}, u32[]{:S(2)}, u32[]{:S(2)}) collective-permute-start(f32[16,8,512]{2,1,0:T(8,128)S(1)} %get-tuple-element.45), channel_id=1, source_target_pairs={{0,8},{8,0},{16,24},{24,16},{32,40},{40,32},{48,56},{56,48},{64,72... | collective-permute-start | bytes 786440 | tf_op jit(solution)/shard_map/ppermute | solution.py:376
  12.0 8.7 %collective-permute-start.1 = (f32[8,8,512]{2,1,0:T(8,128)S(1)}, f32[8,8,512]{2,1,0:T(8,128)S(1)}, u32[]{:S(2)}, u32[]{:S(2)}) collective-permute-start(f32[8,8,512]{2,1,0:T(8,128)S(1)} %get-tuple-element.43), channel_id=1, source_target_pairs={{1,2},{2,1},{3,4},{4,3},{5,6},{6,5},{7,0},{0,7},{9,10},{10,9},{11,... | collective-permute-start | bytes 393224 | tf_op jit(solution)/shard_map/ppermute | solution.py:374
  14.9 5.8 %collective-permute-start.2 = (f32[8,8,512]{2,1,0:T(8,128)S(1)}, f32[8,8,512]{2,1,0:T(8,128)S(1)}, u32[]{:S(2)}, u32[]{:S(2)}) collective-permute-start(f32[8,8,512]{2,1,0:T(8,128)S(1)} %get-tuple-element.44), channel_id=1, source_target_pairs={{0,1},{1,0},{2,3},{3,2},{4,5},{5,4},{6,7},{7,6},{8,9},{9,8},{10,11... | collective-permute-start | bytes 393224 | tf_op jit(solution)/shard_map/ppermute | solution.py:375
  21.1 10.9 %collective-permute-start.4 = (f32[16,8,512]{2,1,0:T(8,128)S(1)}, f32[16,8,512]{2,1,0:T(8,128)S(1)}, u32[]{:S(2)}, u32[]{:S(2)}) collective-permute-start(f32[16,8,512]{2,1,0:T(8,128)S(1)} %get-tuple-element.50), channel_id=1, source_target_pairs={{8,16},{16,8},{24,32},{32,24},{40,48},{48,40},{56,64},{64,56},{72,... | collective-permute-start | bytes 786440 | tf_op jit(solution)/shard_map/ppermute | solution.py:373
  21.2 10.8 %collective-permute-start.7 = (f32[16,8,512]{2,1,0:T(8,128)S(1)}, f32[16,8,512]{2,1,0:T(8,128)S(1)}, u32[]{:S(2)}, u32[]{:S(2)}) collective-permute-start(f32[16,8,512]{2,1,0:T(8,128)S(1)} %get-tuple-element.53), channel_id=1, source_target_pairs={{0,8},{8,0},{16,24},{24,16},{32,40},{40,32},{48,56},{56,48},{64,72... | collective-permute-start | bytes 786440 | tf_op jit(solution)/shard_map/ppermute | solution.py:376
  24.2 7.2 %collective-permute-start.5 = (f32[8,8,512]{2,1,0:T(8,128)S(1)}, f32[8,8,512]{2,1,0:T(8,128)S(1)}, u32[]{:S(2)}, u32[]{:S(2)}) collective-permute-start(f32[8,8,512]{2,1,0:T(8,128)S(1)} %get-tuple-element.51), channel_id=1, source_target_pairs={{1,2},{2,1},{3,4},{4,3},{5,6},{6,5},{7,0},{0,7},{9,10},{10,9},{11,... | collective-permute-start | bytes 393224 | tf_op jit(solution)/shard_map/ppermute | solution.py:374
  27.2 4.8 %collective-permute-start.6 = (f32[8,8,512]{2,1,0:T(8,128)S(1)}, f32[8,8,512]{2,1,0:T(8,128)S(1)}, u32[]{:S(2)}, u32[]{:S(2)}) collective-permute-start(f32[8,8,512]{2,1,0:T(8,128)S(1)} %get-tuple-element.52), channel_id=1, source_target_pairs={{0,1},{1,0},{2,3},{3,2},{4,5},{5,4},{6,7},{7,6},{8,9},{9,8},{10,11... | collective-permute-start | bytes 393224 | tf_op jit(solution)/shard_map/ppermute | solution.py:375
  32.3 12.3 %collective-permute-start.8 = (f32[16,8,512]{2,1,0:T(8,128)S(1)}, f32[16,8,512]{2,1,0:T(8,128)S(1)}, u32[]{:S(2)}, u32[]{:S(2)}) collective-permute-start(f32[16,8,512]{2,1,0:T(8,128)S(1)} %get-tuple-element.60), channel_id=1, source_target_pairs={{8,16},{16,8},{24,32},{32,24},{40,48},{48,40},{56,64},{64,56},{72,... | collective-permute-start | bytes 786440 | tf_op jit(solution)/shard_map/ppermute | solution.py:373
  32.4 12.2 %collective-permute-start.11 = (f32[16,8,512]{2,1,0:T(8,128)S(1)}, f32[16,8,512]{2,1,0:T(8,128)S(1)}, u32[]{:S(2)}, u32[]{:S(2)}) collective-permute-start(f32[16,8,512]{2,1,0:T(8,128)S(1)} %get-tuple-element.63), channel_id=1, source_target_pairs={{0,8},{8,0},{16,24},{24,16},{32,40},{40,32},{48,56},{56,48},{64,72... | collective-permute-start | bytes 786440 | tf_op jit(solution)/shard_map/ppermute | solution.py:376
  36.7 7.8 %collective-permute-start.9 = (f32[8,8,512]{2,1,0:T(8,128)S(1)}, f32[8,8,512]{2,1,0:T(8,128)S(1)}, u32[]{:S(2)}, u32[]{:S(2)}) collective-permute-start(f32[8,8,512]{2,1,0:T(8,128)S(1)} %get-tuple-element.61), channel_id=1, source_target_pairs={{1,2},{2,1},{3,4},{4,3},{5,6},{6,5},{7,0},{0,7},{9,10},{10,9},{11,... | collective-permute-start | bytes 393224 | tf_op jit(solution)/shard_map/ppermute | solution.py:374
  39.3 5.3 %collective-permute-start.10 = (f32[8,8,512]{2,1,0:T(8,128)S(1)}, f32[8,8,512]{2,1,0:T(8,128)S(1)}, u32[]{:S(2)}, u32[]{:S(2)}) collective-permute-start(f32[8,8,512]{2,1,0:T(8,128)S(1)} %get-tuple-element.62), channel_id=1, source_target_pairs={{0,1},{1,0},{2,3},{3,2},{4,5},{5,4},{6,7},{7,6},{8,9},{9,8},{10,11... | collective-permute-start | bytes 393224 | tf_op jit(solution)/shard_map/ppermute | solution.py:375
  51.3 1.5 %collective-permute-start.12 = (f32[1,1152]{1,0:T(1,128)S(1)}, f32[1,1152]{1,0:T(1,128)S(1)}, u32[]{:S(2)}, u32[]{:S(2)}) collective-permute-start(f32[1,1152]{1,0:T(1,128)S(1)} %get-tuple-element.67), channel_id=1, source_target_pairs={{0,8},{8,0},{1,9},{9,1},{2,10},{10,2},{3,11},{11,3},{4,12},{12,4},... | collective-permute-start | bytes 13832 | tf_op jit(solution)/shard_map/ppermute | solution.py:418

commit v2 on v1

v2 whole, which is shorter than its diff:
```python
import jax
import jax.numpy as jnp
from jax import lax
from jax.experimental import pallas as pl
from jax.experimental.pallas import tpu as pltpu
from jax.sharding import Mesh, PartitionSpec as P


COLS = 8
QCOLS = 128
LX = 8
LY = 16
CELLS = LX * LY
NZ = 512
ZT = NZ // 128
STEP = CELLS * ZT
F32 = jnp.float32
BF16 = jnp.bfloat16

GX = ("zh", "y", "core")
GY = ("zl", "x")
CHIPS = ("zh", "y", "zl", "x")

VM = pl.BlockSpec(memory_space=pltpu.VMEM)
HB = pl.BlockSpec(memory_space=pltpu.HBM)
SM = pl.BlockSpec(memory_space=pltpu.SMEM)

FIELD = (CELLS, COLS, NZ)
XFACE = (LY, COLS, NZ)
YFACE = (LX, COLS, NZ)


def sds(shape, dtype=F32):
    return jax.ShapeDtypeStruct(shape, dtype)


def stored(block):
    n = block.shape[0]
    return block.reshape(n, LX, LY // 8, 8, ZT, 128).transpose(0, 1, 2, 4, 3, 5).reshape(n * STEP, 128)


def unstored(rows):
    n = rows.shape[0] // STEP
    return rows.reshape(n, LX, LY // 8, ZT, 8, 128).transpose(0, 1, 2, 4, 3, 5).reshape(n, LX, LY, NZ)


def spot(r):
    return r if isinstance(r, tuple) else (r // 8, lax.rem(r, 8))


def coef(c_ref, k, r):
    t, j = spot(r)
    at = k * STEP + t * 32 + j
    return jnp.concatenate([c_ref[pl.ds(at + zt * 8, COLS, stride=0), :] for zt in range(ZT)], axis=1)


def columns(r_ref, r):
    t, j = spot(r)
    at = t * 32 + j
    return jnp.concatenate([r_ref[pl.ds(at + zt * 8, COLS, stride=STEP), :] for zt in range(ZT)], axis=1)


def put_columns(o_ref, r, v):
    t, j = spot(r)
    at = t * 32 + j
    for zt in range(ZT):
        o_ref[pl.ds(at + zt * 8, COLS, stride=STEP), :] = v[:, zt * 128 : zt * 128 + 128]


def swapped(vs):
    vs = list(vs)
    row = lax.broadcasted_iota(jnp.int32, vs[0].shape, 0)
    for step in (4, 2, 1):
        low = jnp.bitwise_and(row, step) == 0
        for i in range(8):
            if not i & step:
                a, b = vs[i], vs[i + step]
                vs[i] = jnp.where(low, a, pltpu.roll(b, step, 0))
                vs[i + step] = jnp.where(low, pltpu.roll(a, 8 - step, 0), b)
    return vs


def natural(r_ref, c, t):
    at = c * STEP + t * 32
    return jnp.concatenate([r_ref[pl.ds(at + zt * 8, 8), :] for zt in range(ZT)], axis=1)


def put_natural(o_ref, c, t, v):
    at = c * STEP + t * 32
    for zt in range(ZT):
        o_ref[pl.ds(at + zt * 8, 8), :] = v[:, zt * 128 : zt * 128 + 128]


def group(r_ref, t):
    return swapped([natural(r_ref, c, t) for c in range(COLS)])


def wide(v):
    return jnp.concatenate([v] * ZT, axis=1)


def x_row(high, i):
    return jnp.where(high, CELLS - LY, 0) + i


def y_row(high, i):
    return jnp.where(high, LY - 1, 0) + LY * i


def face_sides():
    even_x = lax.axis_index("core") == 0
    even_y = lax.rem(lax.axis_index("x"), 2) == 0
    return jnp.logical_not(even_x), jnp.logical_not(even_y), even_y, even_x


def first_kernel(shift_hbm, r_hbm, c_hbm, sb, sd, sc, sa, prm, rs, cs, shift_ref, sem):
    get_s = pltpu.make_async_copy(shift_hbm, shift_ref, sem.at[42])
    get_s.start()
    edge, inside = [], []
    for n, (far, near, count) in enumerate(((c_hbm, cs, 6), (r_hbm, rs, COLS))):
        for k in range(count):
            for part, (first, rows) in enumerate(((0, 64), (STEP - 64, 64), (64, STEP - 128))):
                at = pl.ds(k * STEP + first, rows)
                copy = pltpu.make_async_copy(far.at[at], near.at[at], sem.at[n * 18 + k * 3 + part])
                (inside if part == 2 else edge).append(copy)
    for copy in edge + inside:
        copy.start()
    get_s.wait()
    row = lax.broadcasted_iota(jnp.int32, (COLS, 128), 0)
    index = jnp.zeros((COLS, 128), F32)
    for c in range(COLS):
        index = jnp.where(row == c, shift_ref[c].astype(F32), index)
    sigma = 0.2 * jnp.exp(jnp.log(jnp.full((COLS, 128), 40.0, F32)) * index / 15.0)
    radius = 12.0 / (12.0 + sigma)
    omega_two = 1.0 / (1.0 - radius * radius / 2.0)
    omega_three = 1.0 / (1.0 - radius * radius * omega_two / 4.0)
    prm[0] = sigma
    prm[1] = omega_two
    prm[2] = omega_three
    prm[3] = jnp.sqrt(2.0 * sigma)
    prm[4] = 2.0 * sigma
    fb, fd, fc, fa = face_sides()
    sigma = wide(sigma)

    def diag_of(r):
        d = coef(cs, 0, r)
        for k in range(1, 6):
            d = d + coef(cs, k, r)
        return d + sigma

    tb, ta = jnp.where(fb, CELLS // 8 - 2, 0), jnp.where(fa, CELLS // 8 - 2, 0)
    for copy in edge:
        copy.wait()
    for half in range(2):
        for out, t in ((sb, tb + half), (sa, ta + half)):
            res = group(rs, t)
            for j in range(8):
                out[half * 8 + j] = res[j] / diag_of((t, j))
    for copy in inside:
        copy.wait()

    def ys(i, _):
        for out, r in ((sd, y_row(fd, i)), (sc, y_row(fc, i))):
            out[i] = columns(rs, r) / diag_of(r)
        return 0

    lax.fori_loop(0, LX, ys, 0, unroll=4)


def couplings(f_ref, cz, t):
    before, v = f_ref[jnp.maximum(8 * t - 1, 0)], f_ref[8 * t]
    for j in range(8):
        after = f_ref[jnp.minimum(8 * t + 8, CELLS - 1) if j == 7 else 8 * t + j + 1]
        total = coef(cz, 4, (t, j)) * pltpu.roll(v, 1, 1)
        total += coef(cz, 5, (t, j)) * pltpu.roll(v, NZ - 1, 1)
        total += coef(cz, 0, (t, j)) * f_ref[8 * jnp.maximum(t - 2, 0) + j]
        total += coef(cz, 1, (t, j)) * f_ref[8 * jnp.minimum(t + 2, CELLS // 8 - 1) + j]
        total += coef(cz, 2, (t, j)) * before
        total += coef(cz, 3, (t, j)) * after
        yield j, 8 * t + j, v, total
        before, v = v, after


def second_kernel(rs, cs, prm, o_hbm, start, rdiag, cz, part, ov, sem):
    load = pltpu.make_async_copy(o_hbm, ov, sem)
    load.start()
    sigma = wide(prm[0])
    row = lax.broadcasted_iota(jnp.int32, (64, 128), 0)
    lane = lax.broadcasted_iota(jnp.int32, (64, 128), 1)
    in32, in8 = lax.rem(row, 32), lax.rem(row, 8)
    outside = (
        None,
        None,
        jnp.logical_and(row < 32, in8 == 0),
        jnp.logical_and(row >= 32, in8 == 7),
        jnp.logical_and(in32 < 8, lane == 0),
        jnp.logical_and(in32 >= 24, lane == 127),
    )
    for k in range(6):
        for x in range(LX):
            rows = pl.ds(k * STEP + x * 64, 64)
            if (k, x) in ((0, 0), (1, LX - 1)):
                cz[rows, :] = jnp.zeros((64, 128), F32)
            elif k < 2:
                cz[rows, :] = cs[rows, :]
            else:
                cz[rows, :] = jnp.where(outside[k], 0.0, cs[rows, :])

    def begin(t, _):
        res = group(rs, t)
        for j in range(8):
            d = coef(cs, 0, (t, j))
            for k in range(1, 6):
                d = d + coef(cs, k, (t, j))
            recip = 1.0 / (d + sigma)
            rdiag[8 * t + j] = recip
            start[8 * t + j] = res[j] * recip
        return 0

    lax.fori_loop(0, CELLS // 8, begin, 0)

    def sweep(t, _):
        for _, r, v, total in couplings(start, cz, t):
            part[r] = v + total * rdiag[r]
        return 0

    lax.fori_loop(0, CELLS // 8, sweep, 0)
    load.wait()


def third_kernel(field, start, rdiag, cz, prm, part):
    omega = wide(prm[1])

    def sweep(t, _):
        for _, r, _, total in couplings(field, cz, t):
            part[r] = start[r] + omega * (total * rdiag[r])
        return 0

    lax.fori_loop(0, CELLS // 8, sweep, 0)


def splat(prm, k, c):
    return jnp.broadcast_to(wide(prm[k, c : c + 1, :]), (8, NZ))


def write_out(solved, rs, prm, fscr, nscr, t):
    for c, s in enumerate(swapped(solved)):
        put_natural(fscr, c, t, splat(prm, 3, c) * s)
        put_natural(nscr, c, t, natural(rs, c, t) - splat(prm, 4, c) * s)


def fourth_kernel(field, second, start, rdiag, rs, cz, prm, part, fscr, nscr, low):
    omega, root = wide(prm[2]), wide(prm[3])

    def sweep(t, _):
        solved = []
        for j, r, _, total in couplings(field, cz, t):
            s = second[r]
            s = s + omega * ((start[r] + total * rdiag[r]) - s)
            part[r] = s
            solved.append(s)
            if j % 2:
                pair = jnp.concatenate([root * solved[j - 1], root * s], axis=0)
                low[pl.ds(pl.multiple_of(64 * t + 8 * (j - 1), 16), 16), :] = pair.astype(BF16)
        write_out(solved, rs, prm, fscr, nscr, t)
        return 0

    lax.fori_loop(0, CELLS // 8, sweep, 0)


def fix_faces(field, rdiag, cs, halos, scale):
    fb, fd, fc, fa = face_sides()
    rb, rd, rc, ra = halos

    def add(r, k, halo):
        v = coef(cs, k, r) * halo
        t, j = spot(r)
        v = v * rdiag[8 * t + j]
        if scale is not None:
            v = v * scale
        field[8 * t + j] += v

    tb, ta = jnp.where(fb, CELLS // 8 - 2, 0), jnp.where(fa, CELLS // 8 - 2, 0)
    kb, kd, kc, ka = jnp.where(fb, 1, 0), jnp.where(fd, 3, 2), jnp.where(fc, 3, 2), jnp.where(fa, 1, 0)
    for half in range(2):
        for j in range(8):
            add((tb + half, j), kb, rb[half * 8 + j])
            add((ta + half, j), ka, ra[half * 8 + j])

    def ys(i, _):
        add(y_row(fd, i), kd, rd[i])
        add(y_row(fc, i), kc, rc[i])
        return 0

    lax.fori_loop(0, LX, ys, 0, unroll=4)


def fix_kernel(which, old, rdiag, cs, prm, rb, rd, rc, ra, field, sb, sd, sc, sa):
    del old
    fix_faces(field, rdiag, cs, (rb, rd, rc, ra), wide(prm[which]) if which else None)
    fb, fd, fc, fa = face_sides()
    sb[...] = field[pl.ds(x_row(fb, 0), LY)]
    sa[...] = field[pl.ds(x_row(fa, 0), LY)]
    for i in range(LX):
        sd[i] = field[y_row(fd, i)]
        sc[i] = field[y_row(fc, i)]


def last_kernel(
    old, old_f, old_n, old_low, rdiag, rs, cs, prm, rb, rd, rc, ra, ov,
    field, fscr, nscr, low, fac_hbm, new_hbm, msg, gq, sem,
):
    del old, old_f, old_n, old_low
    fix_faces(field, rdiag, cs, (rb, rd, rc, ra), wide(prm[2]))
    root, twice = wide(prm[3]), wide(prm[4])

    def put_low(t, j0):
        pair = jnp.concatenate([root * field[8 * t + j0], root * field[8 * t + j0 + 1]], axis=0)
        low[pl.ds(pl.multiple_of(64 * t + 8 * j0, 16), 16), :] = pair.astype(BF16)

    for t in (0, 1, CELLS // 8 - 2, CELLS // 8 - 1):
        write_out([field[8 * t + j] for j in range(8)], rs, prm, fscr, nscr, t)
        for j0 in range(0, 8, 2):
            put_low(t, j0)

    def sides(x, _):
        for t, j, j0 in ((2 * x, 0, 0), (2 * x + 1, 7, 6)):
            put_low(t, j0)
            s = field[8 * t + j]
            put_columns(fscr, (t, j), root * s)
            put_columns(nscr, (t, j), columns(rs, (t, j)) - twice * s)
        return 0

    lax.fori_loop(1, LX - 1, sides, 0, unroll=2)
    put_f = pltpu.make_async_copy(fscr, fac_hbm, sem.at[0])
    put_n = pltpu.make_async_copy(nscr, new_hbm, sem.at[1])
    put_f.start()
    put_n.start()
    block = 128

    def gram(q, _):
        q0 = q * block
        p = None
        for x in range(LX):
            o = ov[pl.ds(q0, block), x].reshape(block * LY, NZ)
            w = low[x * 128 : x * 128 + 128, :]
            d = lax.dot_general(o, w, (((1,), (1,)), ((), ())), preferred_element_type=F32)
            p = d if p is None else p + d
        p = p.reshape(block, LY, 128)
        ysub = lax.broadcasted_iota(jnp.int32, (LY, 128), 0)
        ylane = lax.broadcasted_iota(jnp.int32, (LY, 128), 1) // COLS
        g = jnp.sum(jnp.where((ysub == ylane)[None], p, 0.0), axis=1)
        for shift in (64, 32, 16, 8):
            g = g + pltpu.roll(g, shift, 1)
        gq[pl.ds(pl.multiple_of(q0, block), block), :] = g
        return 0

    lax.fori_loop(0, QCOLS // block, gram, 0)
    g = jnp.transpose(gq[...])
    for c in range(COLS):
        msg[0:1, c * 128 : c * 128 + 128] = g[c : c + 1, :]
    lane = lax.broadcasted_iota(jnp.int32, (1, 128), 1)
    norms = jnp.zeros((1, 128), F32)
    for c in range(COLS):
        parts = [jnp.zeros((8, 128), F32)] * 4
        for i in range(STEP // 8):
            n = nscr[c * STEP + i * 8 : c * STEP + i * 8 + 8, :]
            parts[i % 4] = parts[i % 4] + n * n
        total = jnp.sum(parts[0] + parts[1] + parts[2] + parts[3])
        norms = jnp.where(lane == c, total, norms)
    msg[0:1, COLS * 128 :] = norms
    put_f.wait()
    put_n.wait()


def sum_kernel(parts, gram, norms):
    total = jnp.sum(parts[...], axis=0)
    for c in range(COLS):
        gram[c : c + 1, :] = total[:, c * 128 : c * 128 + 128]
    norms[...] = (total[:, COLS * 128 : COLS * 128 + COLS] / (CELLS * NZ * 128)).reshape(COLS)


LIMIT = pltpu.CompilerParams(vmem_limit_bytes=8 << 20)
SENDS = (sds(XFACE), sds(YFACE), sds(YFACE), sds(XFACE))
ROWS = sds((COLS * STEP, 128))
COEFS = sds((6 * STEP, 128))


def in_hbm(x):
    return pltpu.with_memory_space_constraint(x, pltpu.HBM)


def pairs(n, first):
    out = []
    for i in range(first, n, 2):
        out += [(i, (i + 1) % n), ((i + 1) % n, i)]
    return out


def exchange(sends):
    sb, sd, sc, sa = sends
    rb = lax.ppermute(sb, GX, pairs(16, 1))
    rd = lax.ppermute(sd, GY, pairs(8, 1))
    rc = lax.ppermute(sc, GY, pairs(8, 0))
    ra = lax.ppermute(sa, GX, pairs(16, 0))
    return rb, rd, rc, ra


def local(resid_factor, coefficients, observer, shift_index):
    *sends, prm, rs, cs = pl.pallas_call(
        first_kernel, out_shape=(*SENDS, sds((5, COLS, 128)), ROWS, COEFS), in_specs=[HB] * 3, out_specs=(VM,) * 7,
        scratch_shapes=[pltpu.SMEM((COLS,), jnp.int32), pltpu.SemaphoreType.DMA((43,))], compiler_params=LIMIT, name="first",
    )(in_hbm(shift_index), in_hbm(stored(resid_factor)), in_hbm(stored(coefficients)))
    halos = exchange(sends)
    start, rdiag, cz, part, seen = pl.pallas_call(
        second_kernel,
        out_shape=(sds(FIELD), sds(FIELD), COEFS, sds(FIELD), sds(observer.shape, BF16)),
        in_specs=[VM, VM, VM, HB], out_specs=(VM,) * 5, scratch_shapes=[pltpu.SemaphoreType.DMA],
        compiler_params=LIMIT, name="bulk_second",
    )(rs, cs, prm, in_hbm(observer))

    def fixed(which, part, halos):
        return pl.pallas_call(
            lambda *refs: fix_kernel(which, *refs), out_shape=(sds(FIELD), *SENDS), in_specs=[VM] * 8, out_specs=(VM,) * 5,
            input_output_aliases={0: 0}, compiler_params=LIMIT,
        )(part, rdiag, cs, prm, *halos)

    second, *sends = fixed(0, part, halos)
    halos = exchange(sends)
    part = pl.pallas_call(
        third_kernel, out_shape=sds(FIELD), in_specs=[VM] * 5, out_specs=VM, compiler_params=LIMIT, name="bulk_third",
    )(second, start, rdiag, cz, prm)
    third, *sends = fixed(1, part, halos)
    halos = exchange(sends)
    low = sds((COLS * CELLS, NZ), BF16)
    part, fscr, nscr, low_part = pl.pallas_call(
        fourth_kernel, out_shape=(sds(FIELD), ROWS, ROWS, low), in_specs=[VM] * 7, out_specs=(VM,) * 4,
        compiler_params=LIMIT, name="bulk_fourth",
    )(third, second, start, rdiag, rs, cz, prm)
    *_, fac, new, msg = pl.pallas_call(
        last_kernel,
        out_shape=(sds(FIELD), ROWS, ROWS, low, ROWS, ROWS, sds((1, 9 * 128))),
        in_specs=[VM] * 13, out_specs=(VM, VM, VM, VM, HB, HB, VM), input_output_aliases={0: 0, 1: 1, 2: 2, 3: 3},
        scratch_shapes=[pltpu.VMEM((QCOLS, 128), F32), pltpu.SemaphoreType.DMA((2,))],
        compiler_params=LIMIT, name="last",
    )(part, fscr, nscr, low_part, rdiag, rs, cs, prm, *halos, seen)
    msg = msg + lax.ppermute(msg, "core", [(0, 1), (1, 0)])
    gathered = lax.all_to_all(jnp.broadcast_to(msg, (64,) + msg.shape), CHIPS, 0, 0)
    gram, norms = pl.pallas_call(
        sum_kernel, out_shape=(sds((COLS, 128)), sds((COLS,))), in_specs=[VM], out_specs=(VM, VM), name="total",
    )(pltpu.with_memory_space_constraint(gathered, pltpu.VMEM))
    return unstored(fac), unstored(new), gram, norms


def solution(mesh):
    shape = (2, 4, 2, 2, 4)
    fine = Mesh(mesh.devices.reshape(shape), ("zh", "y", "core", "zl", "x"))
    placed = P(None, GX, GY, None)
    return jax.shard_map(
        local, mesh=fine, in_specs=(placed, placed, placed, P()), out_specs=(placed, placed, P(), P()), check_vma=False
    )
```

time: 73.9 us -> 70.2 us (0.950)
  Pallas kernels: 26.6 us -> 22.4 us
  waiting for transfers between devices: 2.64 us -> 4.55 us
  local copies, waits for them, and re-layouts: 1.97 us -> 0.15 us
    pallas_call x4, Pallas kernels: 15.8 us -> 12.4 us  [the longest x1 5.78 us: local(): pl.pallas_call(second_kernel, out_shape=(sds(FIELD), sds(FIELD), COEFS, s...]
    ppermute x3, waiting for transfers between devices: 1.24 us -> 3 us  [exchange(): rd = lax.ppermute(sd, GY, pairs(8, 1))]
    squeeze x1 -> x0, local copies, waits for them, and re-layouts: 1.17 us -> none  [local(): return (unstored(fac), unstored(new), gram, norms[0, :COLS])]
  transfers between devices with their start and end apart: 13 -> 13, of which waited for: 3 -> 5; matrix products, arithmetic and copies ran while one was open for 0% -> 0% of each run, Pallas kernels for 19% -> 17%
where the time goes in v2:
time: 70.2 us; the launch traced here: 70 us
  starting transfers between devices  24.5 us (35%)
  Pallas kernels  22.4 us (32%)
  blocking collectives  17.6 us (25%)
  waiting for transfers between devices  4.55 us (6%)
  between operations  0.75 us (1%)
    all_to_all x1, blocking collectives, local(): lax.all_to_all(jnp.broadcast_to(msg, (64,) + msg.shape), CHIPS, 0, 0)  17.6 us
    ppermute x3, starting transfers between devices, exchange(): ra = lax.ppermute(sa, GX, pairs(16, 0))  11.9 us
    ppermute x3, starting transfers between devices, exchange(): rd = lax.ppermute(sd, GY, pairs(8, 1))  8.42 us
    pallas_call x1, Pallas kernels, local(): pl.pallas_call(last_kernel, out_shape=(sds(FIELD), ROWS, ROWS, low, ROWS,...  6.63 us
    pallas_call x1, Pallas kernels, local(): pl.pallas_call(second_kernel, out_shape=(sds(FIELD), sds(FIELD), COEFS, s...  5.78 us
    pallas_call x1, Pallas kernels, local(): pl.pallas_call(fourth_kernel, out_shape=(sds(FIELD), ROWS, ROWS, low), in...  3.33 us
    ppermute x3, waiting for transfers between devices, exchange(): rd = lax.ppermute(sd, GY, pairs(8, 1))  3 us
    ppermute x3, starting transfers between devices, exchange(): rb = lax.ppermute(sb, GX, pairs(16, 1))  2.92 us
  transfers between devices with their start and end apart: 13, of which 5 were waited for; matrix products, arithmetic and copies ran while one was open for 0% of the time, Pallas kernels for 17%

profile of v2, /device:TPU:1, one launch (start us, length us, event | category | flops | bytes accessed | tf_op | source)
XLA Modules:
  0.0 70.0 jit_solution(14893865139474800169)
XLA Ops:
  0.6 2.7 %first.1 = (f32[16,8,512]{2,1,0:T(8,128)S(1)}, f32[8,8,512]{2,1,0:T(8,128)S(1)}, f32[8,8,512]{2,1,0:T(8,128)S(1)}, f32[16,8,512]{2,1,0:T(8,128)S(1)}, f32[5,8,12...) custom-call(s32[8]{0:T(128)} %shift_hbm.1, f32[4096,128]{1,0:T(8,128)} %bitcast.20, ...), custom_call_target="tpu_custom_call" | custom-call | tf_op jit(solution)/shard_map/first/pallas_call | solution.py:410
  3.4 2.8 %collective-permute-start = (f32[16,8,512]{2,1,0:T(8,128)S(1)}, f32[16,8,512]{2,1,0:T(8,128)S(1)}, u32[]{:S(2)}, u32[]{:S(2)}) collective-permute-start(f32[16,8,512]{2,1,0:T(8,128)S(1)} %get-tuple-element.40), channel_id=1, source_target_pairs={{8,16},{16,8},{24,32},{32,24},{40,48},{48,40},{56,64},{64,56},{72,... | collective-permute-start | bytes 786440 | tf_op jit(solution)/shard_map/ppermute | solution.py:402
  6.1 4.6 %collective-permute-start.3 = (f32[16,8,512]{2,1,0:T(8,128)S(1)}, f32[16,8,512]{2,1,0:T(8,128)S(1)}, u32[]{:S(2)}, u32[]{:S(2)}) collective-permute-start(f32[16,8,512]{2,1,0:T(8,128)S(1)} %get-tuple-element.43), channel_id=1, source_target_pairs={{0,8},{8,0},{16,24},{24,16},{32,40},{40,32},{48,56},{56,48},{64,72... | collective-permute-start | bytes 786440 | tf_op jit(solution)/shard_map/ppermute | solution.py:405
  10.7 2.9 %collective-permute-start.1 = (f32[8,8,512]{2,1,0:T(8,128)S(1)}, f32[8,8,512]{2,1,0:T(8,128)S(1)}, u32[]{:S(2)}, u32[]{:S(2)}) collective-permute-start(f32[8,8,512]{2,1,0:T(8,128)S(1)} %get-tuple-element.41), channel_id=1, source_target_pairs={{1,2},{2,1},{3,4},{4,3},{5,6},{6,5},{7,0},{0,7},{9,10},{10,9},{11,... | collective-permute-start | bytes 393224 | tf_op jit(solution)/shard_map/ppermute | solution.py:403
  13.7 5.8 %bulk_second.1 = (f32[128,8,512]{2,1,0:T(8,128)S(1)}, f32[128,8,512]{2,1,0:T(8,128)S(1)}, f32[3072,128]{1,0:T(8,128)S(1)}, f32[128,8,512]{2,1,0:T(8,128)S(1)}, bf16[128,8,16,512]{3,2,1,0:T(8,128)(2,1)S(1)}) custom-call(f32[4096,128]{1,0:T(8,128)S(1)} %get-tuple-element.35.rs, f32[3072,128]{1,0:T(8,128)S(1)} %get-tuple-element.36.cs.refs_2_, ...), custom_call_target="tpu_custom_call" | custom-call | tf_op jit(solution)/shard_map/bulk_second/pallas_call | solution.py:415
  19.5 0.3 shard_map.75
  19.9 3.0 %collective-permute-start.7 = (f32[16,8,512]{2,1,0:T(8,128)S(1)}, f32[16,8,512]{2,1,0:T(8,128)S(1)}, u32[]{:S(2)}, u32[]{:S(2)}) collective-permute-start(f32[16,8,512]{2,1,0:T(8,128)S(1)} %get-tuple-element.50), channel_id=1, source_target_pairs={{0,8},{8,0},{16,24},{24,16},{32,40},{40,32},{48,56},{56,48},{64,72... | collective-permute-start | bytes 786440 | tf_op jit(solution)/shard_map/ppermute | solution.py:405
  23.0 2.9 %collective-permute-start.5 = (f32[8,8,512]{2,1,0:T(8,128)S(1)}, f32[8,8,512]{2,1,0:T(8,128)S(1)}, u32[]{:S(2)}, u32[]{:S(2)}) collective-permute-start(f32[8,8,512]{2,1,0:T(8,128)S(1)} %get-tuple-element.48), channel_id=1, source_target_pairs={{1,2},{2,1},{3,4},{4,3},{5,6},{6,5},{7,0},{0,7},{9,10},{10,9},{11,... | collective-permute-start | bytes 393224 | tf_op jit(solution)/shard_map/ppermute | solution.py:403
  25.9 2.5 %bulk_third.1.refs_0_ = f32[128,8,512]{2,1,0:T(8,128)S(1)} custom-call(f32[128,8,512]{2,1,0:T(8,128)S(1)} %get-tuple-element.44.field.second, f32[128,8,512]{2,1,0:T(8,128)S(1)} %get-tuple-element.45.start, f32[128,8,512]{2,1,0:T(8,128)S(1)} %get-tuple-element.39.refs_1_.rdiag, f32[3072,128]{1,0:T(8,128)S(1)} %get-tuple-element.46.cz, ...), custom_call_target="tpu_custom_call" | custom-call | tf_op jit(solution)/shard_map/bulk_third/pallas_call | solution.py:430
  28.4 1.7 %collective-permute-done.5.refs_5_ = f32[8,8,512]{2,1,0:T(8,128)S(1)} collective-permute-done((f32[8,8,512]{2,1,0:T(8,128)S(1)}, f32[8,8,512]{2,1,0:T(8,128)S(1)}, u32[]{:S(2)}, u32[]{:S(2)}) %collective-permute-start.5) | collective-permute-done | bytes 131104 | tf_op jit(solution)/shard_map/ppermute | solution.py:403
  30.1 0.6 collective-permute-done.6.refs_6_
  30.7 0.3 shard_map.76
  31.0 0.1 collective-permute-start.8
  31.1 4.3 %collective-permute-start.11 = (f32[16,8,512]{2,1,0:T(8,128)S(1)}, f32[16,8,512]{2,1,0:T(8,128)S(1)}, u32[]{:S(2)}, u32[]{:S(2)}) collective-permute-start(f32[16,8,512]{2,1,0:T(8,128)S(1)} %get-tuple-element.59), channel_id=1, source_target_pairs={{0,8},{8,0},{16,24},{24,16},{32,40},{40,32},{48,56},{56,48},{64,72... | collective-permute-start | bytes 786440 | tf_op jit(solution)/shard_map/ppermute | solution.py:405
  35.4 2.5 %collective-permute-start.9 = (f32[8,8,512]{2,1,0:T(8,128)S(1)}, f32[8,8,512]{2,1,0:T(8,128)S(1)}, u32[]{:S(2)}, u32[]{:S(2)}) collective-permute-start(f32[8,8,512]{2,1,0:T(8,128)S(1)} %get-tuple-element.57), channel_id=1, source_target_pairs={{1,2},{2,1},{3,4},{4,3},{5,6},{6,5},{7,0},{0,7},{9,10},{10,9},{11,... | collective-permute-start | bytes 393224 | tf_op jit(solution)/shard_map/ppermute | solution.py:403
  38.0 3.3 %bulk_fourth.1 = (f32[128,8,512]{2,1,0:T(8,128)S(1)}, f32[4096,128]{1,0:T(8,128)S(1)}, f32[4096,128]{1,0:T(8,128)S(1)}, bf16[1024,512]{1,0:T(8,128)(2,1)S(1)}) custom-call(f32[128,8,512]{2,1,0:T(8,128)S(1)} %get-tuple-element.51.field, f32[128,8,512]{2,1,0:T(8,128)S(1)} %get-tuple-element.44.field.second, f32[128,8,512]{2,1,0:T(8,128)S(1)} %get-tuple-element.45.start, ...), custom_call_target="tpu_custom_call" | custom-call | tf_op jit(solution)/shard_map/bulk_fourth/pallas_call | solution.py:436
  41.3 1.3 %collective-permute-done.9.rd = f32[8,8,512]{2,1,0:T(8,128)S(1)} collective-permute-done((f32[8,8,512]{2,1,0:T(8,128)S(1)}, f32[8,8,512]{2,1,0:T(8,128)S(1)}, u32[]{:S(2)}, u32[]{:S(2)}) %collective-permute-start.9) | collective-permute-done | bytes 131104 | tf_op jit(solution)/shard_map/ppermute | solution.py:403
  42.6 0.2 collective-permute-done.10.rc
  42.8 6.6 %last.1 = (f32[128,8,512]{2,1,0:T(8,128)S(1)}, f32[4096,128]{1,0:T(8,128)S(1)}, f32[4096,128]{1,0:T(8,128)S(1)}, bf16[1024,512]{1,0:T(8,128)(2,1)S(1)}, f32[4096...) custom-call(f32[128,8,512]{2,1,0:T(8,128)S(1)} %get-tuple-element.52, ...), custom_call_target="tpu_custom_call", output_to_operand_aliasing={{0}: (0, {}), {1}: (1, {}), {2}: (2, {}), {3}: (3, {})} | custom-call | tf_op jit(solution)/shard_map/last/pallas_call | solution.py:440
  49.4 1.2 %collective-permute-start.12 = (f32[1,1152]{1,0:T(1,128)S(1)}, f32[1,1152]{1,0:T(1,128)S(1)}, u32[]{:S(2)}, u32[]{:S(2)}) collective-permute-start(f32[1,1152]{1,0:T(1,128)S(1)} %get-tuple-element.63), channel_id=1, source_target_pairs={{0,8},{8,0},{1,9},{9,1},{2,10},{10,2},{3,11},{11,3},{4,12},{12,4},... | collective-permute-start | bytes 13832 | tf_op jit(solution)/shard_map/ppermute | solution.py:447
  50.6 0.8 %collective-permute-done.12 = f32[1,1152]{1,0:T(1,128)S(1)} collective-permute-done((f32[1,1152]{1,0:T(1,128)S(1)}, f32[1,1152]{1,0:T(1,128)S(1)}, u32[]{:S(2)}, u32[]{:S(2)}) %collective-permute-start.12) | collective-permute-done | bytes 4640 | tf_op jit(solution)/shard_map/ppermute | solution.py:447
  51.5 0.2 broadcast_in_dim.3
  51.6 17.6 %all_to_all.5.parts = f32[64,1,1152]{2,1,0:T(1,128)S(1)} all-to-all(f32[64,1,1152]{2,1,0:T(1,128)S(1)} %broadcast_in_dim.3), channel_id=1, replica_groups=mesh['zh'=2,'y'=4,'core'=2,'zl'=2,'x'=4] {'zh','y','zl','x'}, dimensions={0} | all-to-all | bytes 589824 | tf_op jit(solution)/shard_map/all_to_all | solution.py:448
  69.2 0.8 %total.1 = (f32[8,128]{1,0:T(8,128)}, f32[8]{0:T(128)}) custom-call(f32[64,1,1152]{2,1,0:T(1,128)S(1)} %all_to_all.5.parts), custom_call_target="tpu_custom_call" | custom-call | tf_op jit(solution)/shard_map/total/pallas_call | solution.py:449
  (13 shorter events, 0.1 us)
Async XLA Ops:
  3.4 16.1 %collective-permute-start = (f32[16,8,512]{2,1,0:T(8,128)S(1)}, f32[16,8,512]{2,1,0:T(8,128)S(1)}, u32[]{:S(2)}, u32[]{:S(2)}) collective-permute-start(f32[16,8,512]{2,1,0:T(8,128)S(1)} %get-tuple-element.40), channel_id=1, source_target_pairs={{8,16},{16,8},{24,32},{32,24},{40,48},{48,40},{56,64},{64,56},{72,... | collective-permute-start | bytes 786440 | tf_op jit(solution)/shard_map/ppermute | solution.py:402
  6.1 13.3 %collective-permute-start.3 = (f32[16,8,512]{2,1,0:T(8,128)S(1)}, f32[16,8,512]{2,1,0:T(8,128)S(1)}, u32[]{:S(2)}, u32[]{:S(2)}) collective-permute-start(f32[16,8,512]{2,1,0:T(8,128)S(1)} %get-tuple-element.43), channel_id=1, source_target_pairs={{0,8},{8,0},{16,24},{24,16},{32,40},{40,32},{48,56},{56,48},{64,72... | collective-permute-start | bytes 786440 | tf_op jit(solution)/shard_map/ppermute | solution.py:405
  10.7 8.7 %collective-permute-start.1 = (f32[8,8,512]{2,1,0:T(8,128)S(1)}, f32[8,8,512]{2,1,0:T(8,128)S(1)}, u32[]{:S(2)}, u32[]{:S(2)}) collective-permute-start(f32[8,8,512]{2,1,0:T(8,128)S(1)} %get-tuple-element.41), channel_id=1, source_target_pairs={{1,2},{2,1},{3,4},{4,3},{5,6},{6,5},{7,0},{0,7},{9,10},{10,9},{11,... | collective-permute-start | bytes 393224 | tf_op jit(solution)/shard_map/ppermute | solution.py:403
  13.7 5.8 %collective-permute-start.2 = (f32[8,8,512]{2,1,0:T(8,128)S(1)}, f32[8,8,512]{2,1,0:T(8,128)S(1)}, u32[]{:S(2)}, u32[]{:S(2)}) collective-permute-start(f32[8,8,512]{2,1,0:T(8,128)S(1)} %get-tuple-element.42), channel_id=1, source_target_pairs={{0,1},{1,0},{2,3},{3,2},{4,5},{5,4},{6,7},{7,6},{8,9},{9,8},{10,11... | collective-permute-start | bytes 393224 | tf_op jit(solution)/shard_map/ppermute | solution.py:404
  19.8 10.9 %collective-permute-start.4 = (f32[16,8,512]{2,1,0:T(8,128)S(1)}, f32[16,8,512]{2,1,0:T(8,128)S(1)}, u32[]{:S(2)}, u32[]{:S(2)}) collective-permute-start(f32[16,8,512]{2,1,0:T(8,128)S(1)} %get-tuple-element.47), channel_id=1, source_target_pairs={{8,16},{16,8},{24,32},{32,24},{40,48},{48,40},{56,64},{64,56},{72,... | collective-permute-start | bytes 786440 | tf_op jit(solution)/shard_map/ppermute | solution.py:402
  19.9 10.8 %collective-permute-start.7 = (f32[16,8,512]{2,1,0:T(8,128)S(1)}, f32[16,8,512]{2,1,0:T(8,128)S(1)}, u32[]{:S(2)}, u32[]{:S(2)}) collective-permute-start(f32[16,8,512]{2,1,0:T(8,128)S(1)} %get-tuple-element.50), channel_id=1, source_target_pairs={{0,8},{8,0},{16,24},{24,16},{32,40},{40,32},{48,56},{56,48},{64,72... | collective-permute-start | bytes 786440 | tf_op jit(solution)/shard_map/ppermute | solution.py:405
  23.0 7.2 %collective-permute-start.5 = (f32[8,8,512]{2,1,0:T(8,128)S(1)}, f32[8,8,512]{2,1,0:T(8,128)S(1)}, u32[]{:S(2)}, u32[]{:S(2)}) collective-permute-start(f32[8,8,512]{2,1,0:T(8,128)S(1)} %get-tuple-element.48), channel_id=1, source_target_pairs={{1,2},{2,1},{3,4},{4,3},{5,6},{6,5},{7,0},{0,7},{9,10},{10,9},{11,... | collective-permute-start | bytes 393224 | tf_op jit(solution)/shard_map/ppermute | solution.py:403
  25.9 4.8 %collective-permute-start.6 = (f32[8,8,512]{2,1,0:T(8,128)S(1)}, f32[8,8,512]{2,1,0:T(8,128)S(1)}, u32[]{:S(2)}, u32[]{:S(2)}) collective-permute-start(f32[8,8,512]{2,1,0:T(8,128)S(1)} %get-tuple-element.49), channel_id=1, source_target_pairs={{0,1},{1,0},{2,3},{3,2},{4,5},{5,4},{6,7},{7,6},{8,9},{9,8},{10,11... | collective-permute-start | bytes 393224 | tf_op jit(solution)/shard_map/ppermute | solution.py:404
  31.0 11.7 %collective-permute-start.8 = (f32[16,8,512]{2,1,0:T(8,128)S(1)}, f32[16,8,512]{2,1,0:T(8,128)S(1)}, u32[]{:S(2)}, u32[]{:S(2)}) collective-permute-start(f32[16,8,512]{2,1,0:T(8,128)S(1)} %get-tuple-element.56), channel_id=1, source_target_pairs={{8,16},{16,8},{24,32},{32,24},{40,48},{48,40},{56,64},{64,56},{72,... | collective-permute-start | bytes 786440 | tf_op jit(solution)/shard_map/ppermute | solution.py:402
  31.1 11.6 %collective-permute-start.11 = (f32[16,8,512]{2,1,0:T(8,128)S(1)}, f32[16,8,512]{2,1,0:T(8,128)S(1)}, u32[]{:S(2)}, u32[]{:S(2)}) collective-permute-start(f32[16,8,512]{2,1,0:T(8,128)S(1)} %get-tuple-element.59), channel_id=1, source_target_pairs={{0,8},{8,0},{16,24},{24,16},{32,40},{40,32},{48,56},{56,48},{64,72... | collective-permute-start | bytes 786440 | tf_op jit(solution)/shard_map/ppermute | solution.py:405
  35.4 7.2 %collective-permute-start.9 = (f32[8,8,512]{2,1,0:T(8,128)S(1)}, f32[8,8,512]{2,1,0:T(8,128)S(1)}, u32[]{:S(2)}, u32[]{:S(2)}) collective-permute-start(f32[8,8,512]{2,1,0:T(8,128)S(1)} %get-tuple-element.57), channel_id=1, source_target_pairs={{1,2},{2,1},{3,4},{4,3},{5,6},{6,5},{7,0},{0,7},{9,10},{10,9},{11,... | collective-permute-start | bytes 393224 | tf_op jit(solution)/shard_map/ppermute | solution.py:403
  38.0 4.8 %collective-permute-start.10 = (f32[8,8,512]{2,1,0:T(8,128)S(1)}, f32[8,8,512]{2,1,0:T(8,128)S(1)}, u32[]{:S(2)}, u32[]{:S(2)}) collective-permute-start(f32[8,8,512]{2,1,0:T(8,128)S(1)} %get-tuple-element.58), channel_id=1, source_target_pairs={{0,1},{1,0},{2,3},{3,2},{4,5},{5,4},{6,7},{7,6},{8,9},{9,8},{10,11... | collective-permute-start | bytes 393224 | tf_op jit(solution)/shard_map/ppermute | solution.py:404
  49.4 2.0 %collective-permute-start.12 = (f32[1,1152]{1,0:T(1,128)S(1)}, f32[1,1152]{1,0:T(1,128)S(1)}, u32[]{:S(2)}, u32[]{:S(2)}) collective-permute-start(f32[1,1152]{1,0:T(1,128)S(1)} %get-tuple-element.63), channel_id=1, source_target_pairs={{0,8},{8,0},{1,9},{9,1},{2,10},{10,2},{3,11},{11,3},{4,12},{12,4},... | collective-permute-start | bytes 13832 | tf_op jit(solution)/shard_map/ppermute | solution.py:447

commit v3 on v2

--- a/solution.py
+++ b/solution.py
@@ -113,7 +113,14 @@
     return jnp.logical_not(even_x), jnp.logical_not(even_y), even_y, even_x
 
 
-def first_kernel(shift_hbm, r_hbm, c_hbm, sb, sd, sc, sa, prm, rs, cs, shift_ref, sem):
+def sum_of(cs, r):
+    d = coef(cs, 0, r)
+    for k in range(1, 6):
+        d = d + coef(cs, k, r)
+    return d
+
+
+def first_kernel(shift_hbm, r_hbm, c_hbm, sb, sa, prm, rs, cs, shift_ref, sem):
     get_s = pltpu.make_async_copy(shift_hbm, shift_ref, sem.at[42])
     get_s.start()
     edge, inside = [], []
@@ -139,15 +146,8 @@
     prm[2] = omega_three
     prm[3] = jnp.sqrt(2.0 * sigma)
     prm[4] = 2.0 * sigma
-    fb, fd, fc, fa = face_sides()
+    fb, _, _, fa = face_sides()
     sigma = wide(sigma)
-
-    def diag_of(r):
-        d = coef(cs, 0, r)
-        for k in range(1, 6):
-            d = d + coef(cs, k, r)
-        return d + sigma
-
     tb, ta = jnp.where(fb, CELLS // 8 - 2, 0), jnp.where(fa, CELLS // 8 - 2, 0)
     for copy in edge:
         copy.wait()
@@ -155,13 +155,18 @@
         for out, t in ((sb, tb + half), (sa, ta + half)):
             res = group(rs, t)
             for j in range(8):
-                out[half * 8 + j] = res[j] / diag_of((t, j))
+                out[half * 8 + j] = res[j] / (sum_of(cs, (t, j)) + sigma)
     for copy in inside:
         copy.wait()
 
+
+def first_sides_kernel(rs, cs, prm, sd, sc):
+    _, fd, fc, _ = face_sides()
+    sigma = wide(prm[0])
+
     def ys(i, _):
         for out, r in ((sd, y_row(fd, i)), (sc, y_row(fc, i))):
-            out[i] = columns(rs, r) / diag_of(r)
+            out[i] = columns(rs, r) / (sum_of(cs, r) + sigma)
         return 0
 
     lax.fori_loop(0, LX, ys, 0, unroll=4)
@@ -407,10 +412,15 @@
 
 
 def local(resid_factor, coefficients, observer, shift_index):
-    *sends, prm, rs, cs = pl.pallas_call(
-        first_kernel, out_shape=(*SENDS, sds((5, COLS, 128)), ROWS, COEFS), in_specs=[HB] * 3, out_specs=(VM,) * 7,
+    sb, sa, prm, rs, cs = pl.pallas_call(
+        first_kernel, out_shape=(sds(XFACE), sds(XFACE), sds((5, COLS, 128)), ROWS, COEFS), in_specs=[HB] * 3, out_specs=(VM,) * 5,
         scratch_shapes=[pltpu.SMEM((COLS,), jnp.int32), pltpu.SemaphoreType.DMA((43,))], compiler_params=LIMIT, name="first",
     )(in_hbm(shift_index), in_hbm(stored(resid_factor)), in_hbm(stored(coefficients)))
+    sd, sc = pl.pallas_call(
+        first_sides_kernel, out_shape=(sds(YFACE), sds(YFACE)), in_specs=[VM] * 3, out_specs=(VM, VM),
+        compiler_params=LIMIT, name="sides",
+    )(rs, cs, prm)
+    sends = (sb, sd, sc, sa)
     halos = exchange(sends)
     start, rdiag, cz, part, seen = pl.pallas_call(
         second_kernel,

time: 70.2 us -> 70.3 us (level)
    ppermute x3, starting transfers between devices: 11.9 us -> 10.9 us  [exchange(): ra = lax.ppermute(sa, GX, pairs(16, 0))]
    ppermute x3, starting transfers between devices: 8.42 us -> 9.17 us  [exchange(): rd = lax.ppermute(sd, GY, pairs(8, 1))]
    pallas_call x1 -> x2, Pallas kernels: 2.74 us -> 2.74 us  [the longest x1 2.49 us: local(): pl.pallas_call(first_kernel, out_shape=(sds(XFACE), sds(XFACE), sds((5, C...]
where the time goes in v3:
time: 70.3 us; the launch traced here: 70.1 us
  starting transfers between devices  24.2 us (34%)
  Pallas kernels  22.4 us (32%)
  blocking collectives  17.9 us (25%)
  waiting for transfers between devices  4.55 us (6%)
  between operations  0.76 us (1%)
    all_to_all x1, blocking collectives, local(): lax.all_to_all(jnp.broadcast_to(msg, (64,) + msg.shape), CHIPS, 0, 0)  17.9 us
    ppermute x3, starting transfers between devices, exchange(): ra = lax.ppermute(sa, GX, pairs(16, 0))  10.9 us
    ppermute x3, starting transfers between devices, exchange(): rd = lax.ppermute(sd, GY, pairs(8, 1))  9.17 us
    pallas_call x1, Pallas kernels, local(): pl.pallas_call(last_kernel, out_shape=(sds(FIELD), ROWS, ROWS, low, ROWS,...  6.63 us
    pallas_call x1, Pallas kernels, local(): pl.pallas_call(second_kernel, out_shape=(sds(FIELD), sds(FIELD), COEFS, s...  5.78 us
    pallas_call x1, Pallas kernels, local(): pl.pallas_call(fourth_kernel, out_shape=(sds(FIELD), ROWS, ROWS, low), in...  3.33 us
    ppermute x3, starting transfers between devices, exchange(): rb = lax.ppermute(sb, GX, pairs(16, 1))  2.92 us
    ppermute x3, waiting for transfers between devices, exchange(): rd = lax.ppermute(sd, GY, pairs(8, 1))  2.56 us
  transfers between devices with their start and end apart: 13, of which 5 were waited for; matrix products, arithmetic and copies ran while one was open for 0% of the time, Pallas kernels for 17%

profile of v3, /device:TPU:1, one launch (start us, length us, event | category | flops | bytes accessed | tf_op | source)
XLA Modules:
  0.0 70.1 jit_solution(6220298598775625853)
XLA Ops:
  0.6 2.5 %first.1 = (f32[16,8,512]{2,1,0:T(8,128)S(1)}, f32[16,8,512]{2,1,0:T(8,128)S(1)}, f32[5,8,128]{2,1,0:T(8,128)S(1)}, f32[4096,128]{1,0:T(8,128)S(1)}, f32[3072,128]{1,0:T(8,128)S(1)}) custom-call(s32[8]{0:T(128)} %shift_hbm.1, f32[4096,128]{1,0:T(8,128)} %bitcast.20, f32[3072,128]{1,0:T(8,128)} %bitcast.21), custom_call_target="tpu_custom_call" | custom-call | tf_op jit(solution)/shard_map/first/pallas_call | solution.py:415
  3.1 2.8 %collective-permute-start = (f32[16,8,512]{2,1,0:T(8,128)S(1)}, f32[16,8,512]{2,1,0:T(8,128)S(1)}, u32[]{:S(2)}, u32[]{:S(2)}) collective-permute-start(f32[16,8,512]{2,1,0:T(8,128)S(1)} %get-tuple-element.40), channel_id=1, source_target_pairs={{8,16},{16,8},{24,32},{32,24},{40,48},{48,40},{56,64},{64,56},{72,... | collective-permute-start | bytes 786440 | tf_op jit(solution)/shard_map/ppermute | solution.py:407
  5.9 4.6 %collective-permute-start.3 = (f32[16,8,512]{2,1,0:T(8,128)S(1)}, f32[16,8,512]{2,1,0:T(8,128)S(1)}, u32[]{:S(2)}, u32[]{:S(2)}) collective-permute-start(f32[16,8,512]{2,1,0:T(8,128)S(1)} %get-tuple-element.43), channel_id=1, source_target_pairs={{0,8},{8,0},{16,24},{24,16},{32,40},{40,32},{48,56},{56,48},{64,72... | collective-permute-start | bytes 786440 | tf_op jit(solution)/shard_map/ppermute | solution.py:410
  10.5 0.3 sides.1
  10.7 3.0 %collective-permute-start.1 = (f32[8,8,512]{2,1,0:T(8,128)S(1)}, f32[8,8,512]{2,1,0:T(8,128)S(1)}, u32[]{:S(2)}, u32[]{:S(2)}) collective-permute-start(f32[8,8,512]{2,1,0:T(8,128)S(1)} %get-tuple-element.41), channel_id=1, source_target_pairs={{1,2},{2,1},{3,4},{4,3},{5,6},{6,5},{7,0},{0,7},{9,10},{10,9},{11,... | collective-permute-start | bytes 393224 | tf_op jit(solution)/shard_map/ppermute | solution.py:408
  13.7 5.8 %bulk_second.1 = (f32[128,8,512]{2,1,0:T(8,128)S(1)}, f32[128,8,512]{2,1,0:T(8,128)S(1)}, f32[3072,128]{1,0:T(8,128)S(1)}, f32[128,8,512]{2,1,0:T(8,128)S(1)}, bf16[128,8,16,512]{3,2,1,0:T(8,128)(2,1)S(1)}) custom-call(f32[4096,128]{1,0:T(8,128)S(1)} %get-tuple-element.35.rs, f32[3072,128]{1,0:T(8,128)S(1)} %get-tuple-element.36.cs.refs_2_, ...), custom_call_target="tpu_custom_call" | custom-call | tf_op jit(solution)/shard_map/bulk_second/pallas_call | solution.py:425
  19.6 0.3 shard_map.75
  20.0 2.4 %collective-permute-start.7 = (f32[16,8,512]{2,1,0:T(8,128)S(1)}, f32[16,8,512]{2,1,0:T(8,128)S(1)}, u32[]{:S(2)}, u32[]{:S(2)}) collective-permute-start(f32[16,8,512]{2,1,0:T(8,128)S(1)} %get-tuple-element.50), channel_id=1, source_target_pairs={{0,8},{8,0},{16,24},{24,16},{32,40},{40,32},{48,56},{56,48},{64,72... | collective-permute-start | bytes 786440 | tf_op jit(solution)/shard_map/ppermute | solution.py:410
  22.4 2.9 %collective-permute-start.5 = (f32[8,8,512]{2,1,0:T(8,128)S(1)}, f32[8,8,512]{2,1,0:T(8,128)S(1)}, u32[]{:S(2)}, u32[]{:S(2)}) collective-permute-start(f32[8,8,512]{2,1,0:T(8,128)S(1)} %get-tuple-element.48), channel_id=1, source_target_pairs={{1,2},{2,1},{3,4},{4,3},{5,6},{6,5},{7,0},{0,7},{9,10},{10,9},{11,... | collective-permute-start | bytes 393224 | tf_op jit(solution)/shard_map/ppermute | solution.py:408
  25.3 2.5 %bulk_third.1.refs_0_ = f32[128,8,512]{2,1,0:T(8,128)S(1)} custom-call(f32[128,8,512]{2,1,0:T(8,128)S(1)} %get-tuple-element.44.field.second, f32[128,8,512]{2,1,0:T(8,128)S(1)} %get-tuple-element.45.start, f32[128,8,512]{2,1,0:T(8,128)S(1)} %get-tuple-element.39.refs_1_.rdiag, f32[3072,128]{1,0:T(8,128)S(1)} %get-tuple-element.46.cz, ...), custom_call_target="tpu_custom_call" | custom-call | tf_op jit(solution)/shard_map/bulk_third/pallas_call | solution.py:440
  27.8 1.7 %collective-permute-done.5.refs_5_ = f32[8,8,512]{2,1,0:T(8,128)S(1)} collective-permute-done((f32[8,8,512]{2,1,0:T(8,128)S(1)}, f32[8,8,512]{2,1,0:T(8,128)S(1)}, u32[]{:S(2)}, u32[]{:S(2)}) %collective-permute-start.5) | collective-permute-done | bytes 131104 | tf_op jit(solution)/shard_map/ppermute | solution.py:408
  29.5 0.6 collective-permute-done.6.refs_6_
  30.1 0.3 shard_map.76
  30.5 4.0 %collective-permute-start.11 = (f32[16,8,512]{2,1,0:T(8,128)S(1)}, f32[16,8,512]{2,1,0:T(8,128)S(1)}, u32[]{:S(2)}, u32[]{:S(2)}) collective-permute-start(f32[16,8,512]{2,1,0:T(8,128)S(1)} %get-tuple-element.59), channel_id=1, source_target_pairs={{0,8},{8,0},{16,24},{24,16},{32,40},{40,32},{48,56},{56,48},{64,72... | collective-permute-start | bytes 786440 | tf_op jit(solution)/shard_map/ppermute | solution.py:410
  34.5 3.2 %collective-permute-start.9 = (f32[8,8,512]{2,1,0:T(8,128)S(1)}, f32[8,8,512]{2,1,0:T(8,128)S(1)}, u32[]{:S(2)}, u32[]{:S(2)}) collective-permute-start(f32[8,8,512]{2,1,0:T(8,128)S(1)} %get-tuple-element.57), channel_id=1, source_target_pairs={{1,2},{2,1},{3,4},{4,3},{5,6},{6,5},{7,0},{0,7},{9,10},{10,9},{11,... | collective-permute-start | bytes 393224 | tf_op jit(solution)/shard_map/ppermute | solution.py:408
  37.7 3.3 %bulk_fourth.1 = (f32[128,8,512]{2,1,0:T(8,128)S(1)}, f32[4096,128]{1,0:T(8,128)S(1)}, f32[4096,128]{1,0:T(8,128)S(1)}, bf16[1024,512]{1,0:T(8,128)(2,1)S(1)}) custom-call(f32[128,8,512]{2,1,0:T(8,128)S(1)} %get-tuple-element.51.field, f32[128,8,512]{2,1,0:T(8,128)S(1)} %get-tuple-element.44.field.second, f32[128,8,512]{2,1,0:T(8,128)S(1)} %get-tuple-element.45.start, ...), custom_call_target="tpu_custom_call" | custom-call | tf_op jit(solution)/shard_map/bulk_fourth/pallas_call | solution.py:446
  41.1 0.8 %collective-permute-done.9.rd = f32[8,8,512]{2,1,0:T(8,128)S(1)} collective-permute-done((f32[8,8,512]{2,1,0:T(8,128)S(1)}, f32[8,8,512]{2,1,0:T(8,128)S(1)}, u32[]{:S(2)}, u32[]{:S(2)}) %collective-permute-start.9) | collective-permute-done | bytes 131104 | tf_op jit(solution)/shard_map/ppermute | solution.py:408
  41.9 0.6 collective-permute-done.10.rc
  42.5 6.6 %last.1 = (f32[128,8,512]{2,1,0:T(8,128)S(1)}, f32[4096,128]{1,0:T(8,128)S(1)}, f32[4096,128]{1,0:T(8,128)S(1)}, bf16[1024,512]{1,0:T(8,128)(2,1)S(1)}, f32[4096...) custom-call(f32[128,8,512]{2,1,0:T(8,128)S(1)} %get-tuple-element.52, ...), custom_call_target="tpu_custom_call", output_to_operand_aliasing={{0}: (0, {}), {1}: (1, {}), {2}: (2, {}), {3}: (3, {})} | custom-call | tf_op jit(solution)/shard_map/last/pallas_call | solution.py:450
  49.2 1.2 %collective-permute-start.12 = (f32[1,1152]{1,0:T(1,128)S(1)}, f32[1,1152]{1,0:T(1,128)S(1)}, u32[]{:S(2)}, u32[]{:S(2)}) collective-permute-start(f32[1,1152]{1,0:T(1,128)S(1)} %get-tuple-element.63), channel_id=1, source_target_pairs={{0,8},{8,0},{1,9},{9,1},{2,10},{10,2},{3,11},{11,3},{4,12},{12,4},... | collective-permute-start | bytes 13832 | tf_op jit(solution)/shard_map/ppermute | solution.py:457
  50.4 0.8 %collective-permute-done.12 = f32[1,1152]{1,0:T(1,128)S(1)} collective-permute-done((f32[1,1152]{1,0:T(1,128)S(1)}, f32[1,1152]{1,0:T(1,128)S(1)}, u32[]{:S(2)}, u32[]{:S(2)}) %collective-permute-start.12) | collective-permute-done | bytes 4640 | tf_op jit(solution)/shard_map/ppermute | solution.py:457
  51.2 0.2 broadcast_in_dim.3
  51.4 17.9 %all_to_all.5.parts = f32[64,1,1152]{2,1,0:T(1,128)S(1)} all-to-all(f32[64,1,1152]{2,1,0:T(1,128)S(1)} %broadcast_in_dim.3), channel_id=1, replica_groups=mesh['zh'=2,'y'=4,'core'=2,'zl'=2,'x'=4] {'zh','y','zl','x'}, dimensions={0} | all-to-all | bytes 589824 | tf_op jit(solution)/shard_map/all_to_all | solution.py:458
  69.3 0.8 %total.1 = (f32[8,128]{1,0:T(8,128)}, f32[8]{0:T(128)}) custom-call(f32[64,1,1152]{2,1,0:T(1,128)S(1)} %all_to_all.5.parts), custom_call_target="tpu_custom_call" | custom-call | tf_op jit(solution)/shard_map/total/pallas_call | solution.py:459
  (14 shorter events, 0.2 us)
Async XLA Ops:
  3.1 16.4 %collective-permute-start = (f32[16,8,512]{2,1,0:T(8,128)S(1)}, f32[16,8,512]{2,1,0:T(8,128)S(1)}, u32[]{:S(2)}, u32[]{:S(2)}) collective-permute-start(f32[16,8,512]{2,1,0:T(8,128)S(1)} %get-tuple-element.40), channel_id=1, source_target_pairs={{8,16},{16,8},{24,32},{32,24},{40,48},{48,40},{56,64},{64,56},{72,... | collective-permute-start | bytes 786440 | tf_op jit(solution)/shard_map/ppermute | solution.py:407
  5.9 13.7 %collective-permute-start.3 = (f32[16,8,512]{2,1,0:T(8,128)S(1)}, f32[16,8,512]{2,1,0:T(8,128)S(1)}, u32[]{:S(2)}, u32[]{:S(2)}) collective-permute-start(f32[16,8,512]{2,1,0:T(8,128)S(1)} %get-tuple-element.43), channel_id=1, source_target_pairs={{0,8},{8,0},{16,24},{24,16},{32,40},{40,32},{48,56},{56,48},{64,72... | collective-permute-start | bytes 786440 | tf_op jit(solution)/shard_map/ppermute | solution.py:410
  10.7 8.8 %collective-permute-start.1 = (f32[8,8,512]{2,1,0:T(8,128)S(1)}, f32[8,8,512]{2,1,0:T(8,128)S(1)}, u32[]{:S(2)}, u32[]{:S(2)}) collective-permute-start(f32[8,8,512]{2,1,0:T(8,128)S(1)} %get-tuple-element.41), channel_id=1, source_target_pairs={{1,2},{2,1},{3,4},{4,3},{5,6},{6,5},{7,0},{0,7},{9,10},{10,9},{11,... | collective-permute-start | bytes 393224 | tf_op jit(solution)/shard_map/ppermute | solution.py:408
  13.7 5.8 %collective-permute-start.2 = (f32[8,8,512]{2,1,0:T(8,128)S(1)}, f32[8,8,512]{2,1,0:T(8,128)S(1)}, u32[]{:S(2)}, u32[]{:S(2)}) collective-permute-start(f32[8,8,512]{2,1,0:T(8,128)S(1)} %get-tuple-element.42), channel_id=1, source_target_pairs={{0,1},{1,0},{2,3},{3,2},{4,5},{5,4},{6,7},{7,6},{8,9},{9,8},{10,11... | collective-permute-start | bytes 393224 | tf_op jit(solution)/shard_map/ppermute | solution.py:409
  19.9 10.2 %collective-permute-start.4 = (f32[16,8,512]{2,1,0:T(8,128)S(1)}, f32[16,8,512]{2,1,0:T(8,128)S(1)}, u32[]{:S(2)}, u32[]{:S(2)}) collective-permute-start(f32[16,8,512]{2,1,0:T(8,128)S(1)} %get-tuple-element.47), channel_id=1, source_target_pairs={{8,16},{16,8},{24,32},{32,24},{40,48},{48,40},{56,64},{64,56},{72,... | collective-permute-start | bytes 786440 | tf_op jit(solution)/shard_map/ppermute | solution.py:407
  20.0 10.1 %collective-permute-start.7 = (f32[16,8,512]{2,1,0:T(8,128)S(1)}, f32[16,8,512]{2,1,0:T(8,128)S(1)}, u32[]{:S(2)}, u32[]{:S(2)}) collective-permute-start(f32[16,8,512]{2,1,0:T(8,128)S(1)} %get-tuple-element.50), channel_id=1, source_target_pairs={{0,8},{8,0},{16,24},{24,16},{32,40},{40,32},{48,56},{56,48},{64,72... | collective-permute-start | bytes 786440 | tf_op jit(solution)/shard_map/ppermute | solution.py:410
  22.4 7.2 %collective-permute-start.5 = (f32[8,8,512]{2,1,0:T(8,128)S(1)}, f32[8,8,512]{2,1,0:T(8,128)S(1)}, u32[]{:S(2)}, u32[]{:S(2)}) collective-permute-start(f32[8,8,512]{2,1,0:T(8,128)S(1)} %get-tuple-element.48), channel_id=1, source_target_pairs={{1,2},{2,1},{3,4},{4,3},{5,6},{6,5},{7,0},{0,7},{9,10},{10,9},{11,... | collective-permute-start | bytes 393224 | tf_op jit(solution)/shard_map/ppermute | solution.py:408
  25.3 4.8 %collective-permute-start.6 = (f32[8,8,512]{2,1,0:T(8,128)S(1)}, f32[8,8,512]{2,1,0:T(8,128)S(1)}, u32[]{:S(2)}, u32[]{:S(2)}) collective-permute-start(f32[8,8,512]{2,1,0:T(8,128)S(1)} %get-tuple-element.49), channel_id=1, source_target_pairs={{0,1},{1,0},{2,3},{3,2},{4,5},{5,4},{6,7},{7,6},{8,9},{9,8},{10,11... | collective-permute-start | bytes 393224 | tf_op jit(solution)/shard_map/ppermute | solution.py:409
  30.4 12.1 %collective-permute-start.8 = (f32[16,8,512]{2,1,0:T(8,128)S(1)}, f32[16,8,512]{2,1,0:T(8,128)S(1)}, u32[]{:S(2)}, u32[]{:S(2)}) collective-permute-start(f32[16,8,512]{2,1,0:T(8,128)S(1)} %get-tuple-element.56), channel_id=1, source_target_pairs={{8,16},{16,8},{24,32},{32,24},{40,48},{48,40},{56,64},{64,56},{72,... | collective-permute-start | bytes 786440 | tf_op jit(solution)/shard_map/ppermute | solution.py:407
  30.5 12.0 %collective-permute-start.11 = (f32[16,8,512]{2,1,0:T(8,128)S(1)}, f32[16,8,512]{2,1,0:T(8,128)S(1)}, u32[]{:S(2)}, u32[]{:S(2)}) collective-permute-start(f32[16,8,512]{2,1,0:T(8,128)S(1)} %get-tuple-element.59), channel_id=1, source_target_pairs={{0,8},{8,0},{16,24},{24,16},{32,40},{40,32},{48,56},{56,48},{64,72... | collective-permute-start | bytes 786440 | tf_op jit(solution)/shard_map/ppermute | solution.py:410
  34.5 7.4 %collective-permute-start.9 = (f32[8,8,512]{2,1,0:T(8,128)S(1)}, f32[8,8,512]{2,1,0:T(8,128)S(1)}, u32[]{:S(2)}, u32[]{:S(2)}) collective-permute-start(f32[8,8,512]{2,1,0:T(8,128)S(1)} %get-tuple-element.57), channel_id=1, source_target_pairs={{1,2},{2,1},{3,4},{4,3},{5,6},{6,5},{7,0},{0,7},{9,10},{10,9},{11,... | collective-permute-start | bytes 393224 | tf_op jit(solution)/shard_map/ppermute | solution.py:408
  37.7 4.8 %collective-permute-start.10 = (f32[8,8,512]{2,1,0:T(8,128)S(1)}, f32[8,8,512]{2,1,0:T(8,128)S(1)}, u32[]{:S(2)}, u32[]{:S(2)}) collective-permute-start(f32[8,8,512]{2,1,0:T(8,128)S(1)} %get-tuple-element.58), channel_id=1, source_target_pairs={{0,1},{1,0},{2,3},{3,2},{4,5},{5,4},{6,7},{7,6},{8,9},{9,8},{10,11... | collective-permute-start | bytes 393224 | tf_op jit(solution)/shard_map/ppermute | solution.py:409
  49.2 2.0 %collective-permute-start.12 = (f32[1,1152]{1,0:T(1,128)S(1)}, f32[1,1152]{1,0:T(1,128)S(1)}, u32[]{:S(2)}, u32[]{:S(2)}) collective-permute-start(f32[1,1152]{1,0:T(1,128)S(1)} %get-tuple-element.63), channel_id=1, source_target_pairs={{0,8},{8,0},{1,9},{9,1},{2,10},{10,2},{3,11},{11,3},{4,12},{12,4},... | collective-permute-start | bytes 13832 | tf_op jit(solution)/shard_map/ppermute | solution.py:457
